TPU v7x, 32 devices: a whole 2x2x4 slice. The times are simulated.
32 devices in a mesh: groups: 2 (over y), ta: 4 (over z), gz: 2 (over x), rep: 2 (over core).
Axes of the slice: x: 2, y: 2, z: 4, core: 2. Of those that a mesh axis runs over, the one named last changes fastest.
Arguments:
- gauge_links: float32 [4, 4, 4, 2, 3, 3, 4, 256], P(('groups', 'rep'), 'ta', 'gz'), parts along dimension 0, may hold values from -1 to 1, as said below
- input_field: float32 [4, 4, 4, 2, 3, 3, 4, 256], P(('groups', 'rep'), 'ta', 'gz'), parts along dimension 0, may hold values from -6 to 6
- conv_weights: float32 [4, 4, 9], replicated, may hold values from -1 to 1
- loss_weight: float32 [4, 4, 4, 256], P(('groups', 'rep'), 'ta', 'gz'), parts along dimension 0, may hold values from 0.005 to 18, as said below
Outputs:
- output_field: float32 [4, 4, 4, 2, 3, 3, 4, 256], P(('groups', 'rep'), 'ta', 'gz'), parts along dimension 0
- field_grad: float32 [4, 4, 4, 2, 3, 3, 4, 256], P(('groups', 'rep'), 'ta', 'gz'), parts along dimension 0
- weight_grad: float32 [8, 4, 9], P('groups'), parts along dimension 0
There are 2 independent parts, one for each index of `groups`. A program takes and returns all parts, laid end to end along the dimension named above; an argument that names none is the same for every part. Nothing has to cross between parts.
Inputs may be any that keep to these rules, and one draw needn't show every extreme that they name: `gauge_links`: every link is a special unitary 3x3 matrix. `loss_weight`: positive.
All inputs are finite; a program needn't handle non-finite values.
Results may differ from a plain program's by a relative error of at most 0.00014.
Values sent between devices are 32-bit elements; how exact they have to be, the bound alone decides.
No kernel may reach another device: no remote copies, remote signals or barrier semaphores. Data moves between devices by JAX's collectives and lax.ppermute only.
A program may use at most 128 MiB of HBM per device.

v0:
```python
import jax
import jax.numpy as jnp
import numpy as np
from jax import lax
from jax.experimental import pallas as pl
from jax.experimental.pallas import tpu as pltpu
from jax.sharding import PartitionSpec as P

PLANES = 2
NCH = 4
TERMS = 9
COMPS = 18
HALF = 2
ROWS = HALF * NCH
LANES = 128
LX = 16
FIELD = (PLANES, COMPS, ROWS, LANES)
F32 = jnp.float32


def to_rows(block):
    planes = block.size // (COMPS * ROWS * LANES)
    split = block.reshape(planes, COMPS, NCH, HALF, LANES)
    return split.transpose(0, 1, 3, 2, 4).reshape(planes, COMPS, ROWS, LANES)


def from_rows(rows, shape):
    split = rows.reshape(PLANES, COMPS, HALF, NCH, LANES)
    return split.transpose(0, 1, 3, 2, 4).reshape(shape)


def sublane_index():
    return lax.broadcasted_iota(jnp.int32, (ROWS, LANES), 0)


def lane_index():
    return lax.broadcasted_iota(jnp.int32, (ROWS, LANES), 1)


def pick_rows(value, index):
    return jnp.take_along_axis(value, index, axis=0, mode="promise_in_bounds")


def as_matrix(items):
    return [[[items[p * 9 + r * 3 + c] for c in range(3)] for r in range(3)] for p in range(2)]


def as_items(matrix):
    return [matrix[p][r][c] for p in range(2) for r in range(3) for c in range(3)]


def total(items):
    result = items[0]
    for item in items[1:]:
        result = result + item
    return result


def product(left, right):
    (lr, li), (rr, ri) = left, right
    out = [[], []]
    for r in range(3):
        out[0].append(
            [
                total([lr[r][k] * rr[k][c] for k in range(3)])
                - total([li[r][k] * ri[k][c] for k in range(3)])
                for c in range(3)
            ]
        )
        out[1].append(
            [
                total([lr[r][k] * ri[k][c] for k in range(3)])
                + total([li[r][k] * rr[k][c] for k in range(3)])
                for c in range(3)
            ]
        )
    return out


def product_left_dagger(left, right):
    (lr, li), (rr, ri) = left, right
    out = [[], []]
    for r in range(3):
        out[0].append(
            [
                total([lr[k][r] * rr[k][c] for k in range(3)])
                + total([li[k][r] * ri[k][c] for k in range(3)])
                for c in range(3)
            ]
        )
        out[1].append(
            [
                total([lr[k][r] * ri[k][c] for k in range(3)])
                - total([li[k][r] * rr[k][c] for k in range(3)])
                for c in range(3)
            ]
        )
    return out


def product_right_dagger(left, right):
    (lr, li), (rr, ri) = left, right
    out = [[], []]
    for r in range(3):
        out[0].append(
            [
                total([lr[r][k] * rr[c][k] for k in range(3)])
                + total([li[r][k] * ri[c][k] for k in range(3)])
                for c in range(3)
            ]
        )
        out[1].append(
            [
                total([li[r][k] * rr[c][k] for k in range(3)])
                - total([lr[r][k] * ri[c][k] for k in range(3)])
                for c in range(3)
            ]
        )
    return out


def hop_forward(link, items):
    matrix = as_matrix(items)
    return as_items(product_right_dagger(product(link, matrix), link))


def hop_backward(link, items):
    matrix = as_matrix(items)
    return as_items(product(product_left_dagger(link, matrix), link))


def load_items(ref, plane):
    return [ref[plane, comp] for comp in range(COMPS)]


def load_link(ref, plane, direction):
    index = (sublane_index() & 4) + direction
    return as_matrix([pick_rows(ref[plane, comp], index) for comp in range(COMPS)])


def load_sent_link(ref, plane):
    base = lax.shift_right_logical(sublane_index(), 2)
    items = []
    for comp in range(COMPS):
        row = (plane * COMPS + comp) * HALF
        start = row // ROWS * ROWS
        items.append(pick_rows(ref[start : start + ROWS, :], base + (row - start)))
    return as_matrix(items)


def step_plane(value, direction, offset):
    lane = lane_index()
    if direction == 3:
        inner = lane & (LX - 1)
        if offset > 0:
            return jnp.where(
                inner == LX - 1,
                pltpu.roll(value, LX - 1, axis=1),
                pltpu.roll(value, LANES - 1, axis=1),
            )
        return jnp.where(
            inner == 0,
            pltpu.roll(value, LANES - LX + 1, axis=1),
            pltpu.roll(value, 1, axis=1),
        )
    if offset > 0:
        moved = pltpu.roll(value, LANES - LX, axis=1)
        return jnp.where(lane >= LANES - LX, pltpu.roll(moved, NCH, axis=0), moved)
    moved = pltpu.roll(value, LX, axis=1)
    return jnp.where(lane < LX, pltpu.roll(moved, NCH, axis=0), moved)


def step_items(items, direction, offset):
    return [step_plane(item, direction, offset) for item in items]


def turned(value):
    sub = sublane_index()
    return [value] + [pick_rows(value, (sub & 4) | ((sub + d) & 3)) for d in range(1, NCH)]


def weight_rows(ref, base, term):
    first = base + term * NCH
    return [
        jnp.broadcast_to(ref[:, first + d : first + d + 1], (ROWS, LANES)) for d in range(NCH)
    ]


def mixed_item(weights, turns):
    return total([weights[d] * turns[d] for d in range(NCH)])


def mixed_items(weights, items):
    return [mixed_item(weights, turned(item)) for item in items]


FORWARD = 0
BACKWARD = TERMS * NCH


def near_forward(field, links, weights, partial, terms):
    for plane in range(PLANES):
        items = load_items(field, plane)
        sums = mixed_items(weight_rows(weights, FORWARD, 0), items)

        def add(term, hop, slot):
            mixed = mixed_items(weight_rows(weights, FORWARD, term), hop)
            for comp in range(COMPS):
                terms[slot, plane, comp] = hop[comp]
                sums[comp] = sums[comp] + mixed[comp]

        for direction in (2, 3):
            link = load_link(links, plane, direction)
            slot = 2 * (direction - 2)
            add(
                2 * direction + 1,
                hop_forward(link, step_items(items, direction, 1)),
                slot,
            )
            add(
                2 * direction + 2,
                step_items(hop_backward(link, items), direction, -1),
                slot + 1,
            )
        link = load_link(links, 0, 1)
        other = load_items(field, 1 - plane)
        if plane == 0:
            add(3, hop_forward(link, other), 4)
        else:
            add(4, hop_backward(link, other), 4)
        for comp in range(COMPS):
            partial[plane, comp] = sums[comp]


def far_forward(
    links, weights, loss, partial, t_next, t_prev, t_link, z_field, z_link, out, cot, terms
):
    for plane in range(PLANES):
        sums = load_items(partial, plane)

        def add(term, hop, slot):
            mixed = mixed_items(weight_rows(weights, FORWARD, term), hop)
            for comp in range(COMPS):
                terms[slot, plane, comp] = hop[comp]
                sums[comp] = sums[comp] + mixed[comp]

        if plane == 0:
            add(4, hop_backward(load_sent_link(z_link, 0), load_items(z_field, 1)), 2)
        else:
            add(3, hop_forward(load_link(links, 1, 1), load_items(z_field, 0)), 2)
        add(1, hop_forward(load_link(links, plane, 0), load_items(t_next, plane)), 0)
        add(2, hop_backward(load_sent_link(t_link, plane), load_items(t_prev, plane)), 1)
        row = loss[plane : plane + 1, :]
        scale = jnp.where(
            sublane_index() < NCH,
            jnp.broadcast_to(row[:, :LANES], (ROWS, LANES)),
            jnp.broadcast_to(row[:, LANES:], (ROWS, LANES)),
        )
        for comp in range(COMPS):
            out[plane, comp] = sums[comp]
            cot[plane, comp] = scale * sums[comp]


def term_item(field, near, far, term, plane, comp):
    if term == 0:
        return field[plane, comp]
    if term >= 5:
        return near[term - 5, plane, comp]
    if term <= 2:
        return far[term - 1, plane, comp]
    if (term == 3) == (plane == 0):
        return near[4, plane, comp]
    return far[2, plane, comp]


def weight_sums(field, cot, near, far, sums, spread):
    sub = sublane_index()
    lane = lane_index()
    for channel in range(NCH):
        index = (sub & 4) + channel
        for plane in range(PLANES):
            for comp in range(COMPS):
                spread[channel, plane, comp] = pick_rows(cot[plane, comp], index)
    rows = [jnp.zeros((ROWS, LANES), F32) for _ in range(NCH)]
    for term in range(TERMS):
        parts = [None] * NCH
        for plane in range(PLANES):
            for comp in range(COMPS):
                value = term_item(field, near, far, term, plane, comp)
                for channel in range(NCH):
                    piece = spread[channel, plane, comp] * value
                    parts[channel] = piece if parts[channel] is None else parts[channel] + piece
        for channel in range(NCH):
            summed = jnp.sum(parts[channel], axis=1, keepdims=True)
            rows[channel] = jnp.where(lane == term, summed, rows[channel])
    for channel in range(NCH):
        both = rows[channel] + pltpu.roll(rows[channel], NCH, axis=0)
        sums[channel] = both[:NCH, :TERMS]


def near_backward(field, links, weights, cot, near, far, sums, partial, spread):
    weight_sums(field, cot, near, far, sums, spread)
    for plane in range(PLANES):
        turns = [turned(cot[plane, comp]) for comp in range(COMPS)]

        def mixed(term):
            rows = weight_rows(weights, BACKWARD, term)
            return [mixed_item(rows, turn) for turn in turns]

        grads = mixed(0)

        def add(hop):
            for comp in range(COMPS):
                grads[comp] = grads[comp] + hop[comp]

        for direction in (2, 3):
            link = load_link(links, plane, direction)
            pulled = hop_backward(link, mixed(2 * direction + 1))
            add(step_items(pulled, direction, -1))
            add(hop_forward(link, step_items(mixed(2 * direction + 2), direction, 1)))
        for comp in range(COMPS):
            partial[plane, comp] = grads[comp]
    link = load_link(links, 0, 1)
    hop = hop_forward(link, mixed_items(weight_rows(weights, BACKWARD, 4), load_items(cot, 1)))
    for comp in range(COMPS):
        partial[0, comp] = partial[0, comp] + hop[comp]
    hop = hop_backward(link, mixed_items(weight_rows(weights, BACKWARD, 3), load_items(cot, 0)))
    for comp in range(COMPS):
        partial[1, comp] = partial[1, comp] + hop[comp]


def far_backward(links, weights, partial, t_next, t_prev, t_link, z_cot, z_link, grad):
    for plane in range(PLANES):
        grads = load_items(partial, plane)

        def mixed(term, ref, source):
            return mixed_items(weight_rows(weights, BACKWARD, term), load_items(ref, source))

        def add(hop):
            for comp in range(COMPS):
                grads[comp] = grads[comp] + hop[comp]

        if plane == 0:
            add(hop_backward(load_sent_link(z_link, 0), mixed(3, z_cot, 1)))
        else:
            add(hop_forward(load_link(links, 1, 1), mixed(4, z_cot, 0)))
        add(hop_forward(load_link(links, plane, 0), mixed(2, t_next, plane)))
        add(hop_backward(load_sent_link(t_link, plane), mixed(1, t_prev, plane)))
        for comp in range(COMPS):
            grad[plane, comp] = grads[comp]


def run(kernel, shapes, *operands, scratch=()):
    outs = [jax.ShapeDtypeStruct(shape, F32) for shape in shapes]
    return pl.pallas_call(
        kernel,
        out_shape=outs,
        scratch_shapes=list(scratch),
        compiler_params=pltpu.CompilerParams(vmem_limit_bytes=32 * 2**20),
    )(*operands)


def shifted(value, axis, offset):
    count = lax.axis_size(axis)
    return lax.ppermute(value, axis, [(i, (i + offset) % count) for i in range(count)])


def z_planes(block):
    if lax.axis_size("gz") == 2:
        return shifted(block, "gz", 1)
    return jnp.concatenate([shifted(block[:1], "gz", -1), shifted(block[1:], "gz", 1)], axis=0)


def summed_over(value, axes):
    for axis in axes:
        count = lax.axis_size(axis)
        if count & (count - 1):
            value = lax.psum(value, axis)
            continue
        step = 1
        while step < count:
            value = value + lax.ppermute(value, axis, [(i, i ^ step) for i in range(count)])
            step *= 2
    return value


def weight_table(conv_weights):
    out_index, in_index, turn = np.indices((NCH, NCH, NCH))
    forward_pick = ((out_index + turn) % NCH == in_index).astype(np.float32)
    backward_pick = ((in_index + turn) % NCH == out_index).astype(np.float32)
    wide = conv_weights[:, :, :, None]
    forward = jnp.sum(wide * forward_pick[:, :, None, :], axis=1)
    backward = jnp.sum(wide * backward_pick[:, :, None, :], axis=0)
    table = jnp.concatenate(
        [forward.reshape(NCH, TERMS * NCH), backward.reshape(NCH, TERMS * NCH)], axis=1
    )
    return jnp.concatenate([table, table], axis=0)


def local(gauge_links, input_field, conv_weights, loss_weight):
    shape = input_field.shape
    field = to_rows(input_field)
    links = to_rows(gauge_links)
    t_link = gauge_links[:, :, :, :, :, :, 0].reshape(PLANES * COMPS * HALF, LANES)
    z_link = gauge_links[:, :, 1, :, :, :, 1].reshape(COMPS * HALF, LANES)
    z_field = z_planes(field)
    t_next = shifted(field, "ta", -1)
    t_prev = shifted(field, "ta", 1)
    z_link = shifted(z_link, "gz", 1)
    t_link = shifted(t_link, "ta", 1)
    weights = weight_table(conv_weights)
    loss = loss_weight.reshape(PLANES, HALF * LANES)
    partial, near = run(near_forward, (FIELD, (5,) + FIELD), field, links, weights)
    out, cot, far = run(
        far_forward,
        (FIELD, FIELD, (3,) + FIELD),
        links,
        weights,
        loss,
        partial,
        t_next,
        t_prev,
        t_link,
        z_field,
        z_link,
    )
    z_cot = z_planes(cot)
    t_next_cot = shifted(cot, "ta", -1)
    t_prev_cot = shifted(cot, "ta", 1)
    sums, grad_partial = run(
        near_backward,
        ((NCH, NCH, TERMS), FIELD),
        field,
        links,
        weights,
        cot,
        near,
        far,
        scratch=[pltpu.VMEM((NCH,) + FIELD, F32)],
    )
    sums = summed_over(sums, ("rep", "gz", "ta"))
    count = loss_weight.size
    for axis in ("ta", "gz", "rep"):
        count = count * lax.axis_size(axis)
    weight_grad = sums / count
    (grad,) = run(
        far_backward,
        (FIELD,),
        links,
        weights,
        grad_partial,
        t_next_cot,
        t_prev_cot,
        t_link,
        z_cot,
        z_link,
    )
    return from_rows(out, shape), from_rows(grad, shape), weight_grad


def solution(mesh):
    split = P(("groups", "rep"), "ta", "gz", None, None, None, None, None)
    return jax.shard_map(
        local,
        mesh=mesh,
        in_specs=(split, split, P(), P(("groups", "rep"), "ta", "gz", None)),
        out_specs=(split, split, P("groups", None, None)),
        check_vma=False,
    )
```

profile of v0, /device:TPU:0, one launch (start us, length us, event | category | flops | bytes accessed | tf_op | source)
XLA Modules:
  0.0 38.5 jit_solution(1174763190038257112)
XLA Ops:
  0.6 3.0 %collective-permute-start.3 = (f32[2,18,8,128]{3,2,1,0:T(8,128)}, f32[2,18,8,128]{3,2,1,0:T(8,128)S(1)}, u32[]{:S(2)}, u32[]{:S(2)}) collective-permute-start(f32[2,18,8,128]{3,2,1,0:T(8,128)} %bitcast.26), channel_id=1, source_target_pairs={{0,2},{2,0},{1,3},{3,1},{4,6},{6,4},{5,7},{7,5},{8,10},{10,8},{9,1... | collective-permute-start | bytes 442376 | tf_op jit(solution)/shard_map/ppermute | solution.py:365
  3.6 1.6 %collective-permute-start.1 = (f32[2,18,8,128]{3,2,1,0:T(8,128)}, f32[2,18,8,128]{3,2,1,0:T(8,128)S(1)}, u32[]{:S(2)}, u32[]{:S(2)}) collective-permute-start(f32[2,18,8,128]{3,2,1,0:T(8,128)} %bitcast.27), channel_id=1, source_target_pairs={{0,4},{4,8},{8,12},{12,0},{1,5},{5,9},{9,13},{13,1},{2,6},{6,10},{... | collective-permute-start | bytes 442376 | tf_op jit(solution)/shard_map/ppermute | solution.py:365
  5.2 2.2 %collective-permute-start = (f32[2,18,8,128]{3,2,1,0:T(8,128)}, f32[2,18,8,128]{3,2,1,0:T(8,128)S(1)}, u32[]{:S(2)}, u32[]{:S(2)}) collective-permute-start(f32[2,18,8,128]{3,2,1,0:T(8,128)} %bitcast.28), channel_id=1, source_target_pairs={{0,12},{4,0},{8,4},{12,8},{1,13},{5,1},{9,5},{13,9},{2,14},{6,2},{... | collective-permute-start | bytes 442376 | tf_op jit(solution)/shard_map/ppermute | solution.py:365
  7.5 0.0 copy-start.3
  7.5 0.0 copy-start.4
  7.5 0.0 copy-start.5
  7.5 1.0 %slice_reduce_fusion = f32[2,3,3,256]{3,2,1,0:T(4,128)S(1)} fusion(f32[1,1,2,2,3,3,4,256]{7,6,5,4,3,2,1,0:T(4,128)} %param.6), kind=kLoop, calls=%fused_computation.2 | loop fusion | bytes 36864 | tf_op jit(solution)/shard_map/slice | solution.py:405
  8.4 0.0 copy-start.1
  8.5 0.0 copy-start
  8.5 0.4 collective-permute-start.4
  8.9 0.9 %slice.6 = f32[1,1,2,2,3,3,1,256]{7,6,5,4,3,2,1,0:T(1,128)S(1)} slice(f32[1,1,2,2,3,3,4,256]{7,6,5,4,3,2,1,0:T(4,128)} %param.6), slice={[0:1], [0:1], [0:2], [0:2], [0:3], [0:3], [0:1], [0:256]} | slice | bytes 73728 | tf_op jit(solution)/shard_map/slice | solution.py:404
  9.8 0.1 collective-permute-start.2
  9.9 0.0 copy-done.3
  9.9 0.0 copy-done.4
  9.9 0.0 copy-done.5
  9.9 0.1 multiply_reduce_fusion.1
  10.0 0.1 copy.18
  10.1 0.1 reshape.42
  10.2 0.1 copy.19
  10.3 0.1 reshape.43
  10.4 0.1 maximum_maximum_fusion.weights
  10.5 0.0 copy-done.1
  10.5 0.0 copy-done
  10.5 1.0 %shard_map.85 = (f32[2,18,8,128]{3,2,1,0:T(8,128)S(1)}, f32[5,2,18,8,128]{4,3,2,1,0:T(8,128)S(1)}) custom-call(f32[2,18,8,128]{3,2,1,0:T(8,128)S(1)} %bitcast.29, f32[2,18,8,128]{3,2,1,0:T(8,128)S(1)} %bitcast.22, f32[8,72]{1,0:T(8,128)S(1)} %maximum_maximum_fusion.weights), custom_call_target="tpu_custom_call" | custom-call | tf_op jit(solution)/shard_map/pallas_call | solution.py:355
  11.5 0.0 copy-start.2
  11.5 0.8 %collective-permute-done.4.z_link = f32[36,128]{1,0:T(8,128)S(1)} collective-permute-done((f32[36,128]{1,0:T(8,128)S(1)}, f32[36,128]{1,0:T(8,128)S(1)}, u32[]{:S(2)}, u32[]{:S(2)}) %collective-permute-start.4) | collective-permute-done | bytes 18464 | tf_op jit(solution)/shard_map/ppermute | solution.py:365
  12.3 3.3 %collective-permute-done.2.t_link = f32[72,128]{1,0:T(8,128)S(1)} collective-permute-done((f32[72,128]{1,0:T(8,128)S(1)}, f32[72,128]{1,0:T(8,128)S(1)}, u32[]{:S(2)}, u32[]{:S(2)}) %collective-permute-start.2) | collective-permute-done | bytes 36896 | tf_op jit(solution)/shard_map/ppermute | solution.py:365
  15.6 0.0 collective-permute-done.3.z_field
  15.6 0.0 collective-permute-done.1.t_prev
  15.6 0.0 collective-permute-done.t_next
  15.6 0.0 copy-done.2
  15.6 1.2 %shard_map.86 = (f32[2,18,8,128]{3,2,1,0:T(8,128)}, f32[2,18,8,128]{3,2,1,0:T(8,128)S(1)}, f32[3,2,18,8,128]{4,3,2,1,0:T(8,128)S(1)}) custom-call(f32[2,18,8,128]{3,2,1,0:T(8,128)S(1)} %bitcast.23, f32[8,72]{1,0:T(8,128)S(1)} %maximum_maximum_fusion.weights, f32[2,256]{1,0:T(2,128)S(1)} %bitcast.31, f32[2,18,8,128]{3,2,1,0:T(8,128)S(1)} %get-tuple-element.10.partial, ...), custom_call_target="tpu_custom_call" | custom-call | tf_op jit(solution)/shard_map/pallas_call | solution.py:355
  16.8 1.9 %shard_map.87 = (f32[4,4,9]{2,1,0:T(4,128)S(1)}, f32[2,18,8,128]{3,2,1,0:T(8,128)S(1)}) custom-call(f32[2,18,8,128]{3,2,1,0:T(8,128)S(1)} %bitcast.30, f32[2,18,8,128]{3,2,1,0:T(8,128)S(1)} %bitcast.24, f32[8,72]{1,0:T(8,128)S(1)} %maximum_maximum_fusion.weights, f32[2,18,8,128]{3,2,1,0:T(8,128)S(1)} %get-tuple-element.12.cot, ...), custom_call_target="tpu_custom_call" | custom-call | tf_op jit(solution)/shard_map/pallas_call | solution.py:355
  18.8 0.1 collective-permute-start.8
  18.8 1.2 %collective-permute-done.8 = f32[4,4,9]{2,1,0:T(4,128)S(1)} collective-permute-done((f32[4,4,9]{2,1,0:T(4,128)S(1)}, f32[4,4,9]{2,1,0:T(4,128)S(1)}, u32[]{:S(2)}, u32[]{:S(2)}) %collective-permute-start.8) | collective-permute-done | bytes 608 | tf_op jit(solution)/shard_map/ppermute | solution.py:382
  20.0 1.7 %collective-permute-start.9 = (f32[4,4,9]{2,1,0:T(4,128)S(1)}, f32[4,4,9]{2,1,0:T(4,128)S(1)}, u32[]{:S(2)}, u32[]{:S(2)}) collective-permute-start(f32[4,4,9]{2,1,0:T(4,128)S(1)} %add.12), channel_id=1, source_target_pairs={{0,2},{2,0},{1,3},{3,1},{4,6},{6,4},{5,7},{7,5},{8,10},{10,8},{9,1... | collective-permute-start | bytes 1736 | tf_op jit(solution)/shard_map/ppermute | solution.py:382
  21.7 1.9 %collective-permute-done.9 = f32[4,4,9]{2,1,0:T(4,128)S(1)} collective-permute-done((f32[4,4,9]{2,1,0:T(4,128)S(1)}, f32[4,4,9]{2,1,0:T(4,128)S(1)}, u32[]{:S(2)}, u32[]{:S(2)}) %collective-permute-start.9) | collective-permute-done | bytes 608 | tf_op jit(solution)/shard_map/ppermute | solution.py:382
  23.7 0.0 collective-permute-start.10
  23.7 3.6 %collective-permute-done.10 = f32[4,4,9]{2,1,0:T(4,128)S(1)} collective-permute-done((f32[4,4,9]{2,1,0:T(4,128)S(1)}, f32[4,4,9]{2,1,0:T(4,128)S(1)}, u32[]{:S(2)}, u32[]{:S(2)}) %collective-permute-start.10) | collective-permute-done | bytes 608 | tf_op jit(solution)/shard_map/ppermute | solution.py:382
  27.3 0.1 collective-permute-start.11
  27.4 1.7 %collective-permute-start.7 = (f32[2,18,8,128]{3,2,1,0:T(8,128)S(1)}, f32[2,18,8,128]{3,2,1,0:T(8,128)S(1)}, u32[]{:S(2)}, u32[]{:S(2)}) collective-permute-start(f32[2,18,8,128]{3,2,1,0:T(8,128)S(1)} %get-tuple-element.12.cot), channel_id=1, source_target_pairs={{0,2},{2,0},{1,3},{3,1},{4,6},{6,4},{5,7},{7,5},{8,10},{10,8},{9,1... | collective-permute-start | bytes 442376 | tf_op jit(solution)/shard_map/ppermute | solution.py:365
  29.1 0.8 %collective-permute-start.6 = (f32[2,18,8,128]{3,2,1,0:T(8,128)S(1)}, f32[2,18,8,128]{3,2,1,0:T(8,128)S(1)}, u32[]{:S(2)}, u32[]{:S(2)}) collective-permute-start(f32[2,18,8,128]{3,2,1,0:T(8,128)S(1)} %get-tuple-element.12.cot), channel_id=1, source_target_pairs={{0,4},{4,8},{8,12},{12,0},{1,5},{5,9},{9,13},{13,1},{2,6},{6,10},{... | collective-permute-start | bytes 442376 | tf_op jit(solution)/shard_map/ppermute | solution.py:365
  29.9 3.0 %collective-permute-start.5 = (f32[2,18,8,128]{3,2,1,0:T(8,128)S(1)}, f32[2,18,8,128]{3,2,1,0:T(8,128)S(1)}, u32[]{:S(2)}, u32[]{:S(2)}) collective-permute-start(f32[2,18,8,128]{3,2,1,0:T(8,128)S(1)} %get-tuple-element.12.cot), channel_id=1, source_target_pairs={{0,12},{4,0},{8,4},{12,8},{1,13},{5,1},{9,5},{13,9},{2,14},{6,2},{... | collective-permute-start | bytes 442376 | tf_op jit(solution)/shard_map/ppermute | solution.py:365
  32.9 0.0 collective-permute-done.11
  32.9 0.6 %add_multiply_fusion = f32[4,4,9]{2,1,0:T(4,128)} fusion(f32[4,4,9]{2,1,0:T(4,128)S(1)} %add.14, f32[4,4,9]{2,1,0:T(4,128)S(1)} %collective-permute-done.11), kind=kLoop, calls=%fused_computation.3 | loop fusion | flops 288 | bytes 1728 | tf_op jit(solution)/shard_map/div | solution.py:445
  33.5 0.0 collective-permute-done.7.z_cot
  33.5 2.6 %collective-permute-done.6.t_prev = f32[2,18,8,128]{3,2,1,0:T(8,128)S(1)} collective-permute-done((f32[2,18,8,128]{3,2,1,0:T(8,128)S(1)}, f32[2,18,8,128]{3,2,1,0:T(8,128)S(1)}, u32[]{:S(2)}, u32[]{:S(2)}) %collective-permute-start.6) | collective-permute-done | bytes 147488 | tf_op jit(solution)/shard_map/ppermute | solution.py:365
  36.2 1.0 %collective-permute-done.5.t_next = f32[2,18,8,128]{3,2,1,0:T(8,128)S(1)} collective-permute-done((f32[2,18,8,128]{3,2,1,0:T(8,128)S(1)}, f32[2,18,8,128]{3,2,1,0:T(8,128)S(1)}, u32[]{:S(2)}, u32[]{:S(2)}) %collective-permute-start.5) | collective-permute-done | bytes 147488 | tf_op jit(solution)/shard_map/ppermute | solution.py:365
  37.2 1.3 %shard_map.88 = f32[2,18,8,128]{3,2,1,0:T(8,128)} custom-call(f32[2,18,8,128]{3,2,1,0:T(8,128)S(1)} %bitcast.25, f32[8,72]{1,0:T(8,128)S(1)} %maximum_maximum_fusion.weights, f32[2,18,8,128]{3,2,1,0:T(8,128)S(1)} %get-tuple-element.15.partial, f32[2,18,8,128]{3,2,1,0:T(8,128)S(1)} %collective-permute-done.5.t_next, ...), custom_call_target="tpu_custom_call" | custom-call | tf_op jit(solution)/shard_map/pallas_call | solution.py:355
  (4 shorter events, 0.0 us)
Async XLA Ops:
  0.6 15.0 %collective-permute-start.3 = (f32[2,18,8,128]{3,2,1,0:T(8,128)}, f32[2,18,8,128]{3,2,1,0:T(8,128)S(1)}, u32[]{:S(2)}, u32[]{:S(2)}) collective-permute-start(f32[2,18,8,128]{3,2,1,0:T(8,128)} %bitcast.26), channel_id=1, source_target_pairs={{0,2},{2,0},{1,3},{3,1},{4,6},{6,4},{5,7},{7,5},{8,10},{10,8},{9,1... | collective-permute-start | bytes 442376 | tf_op jit(solution)/shard_map/ppermute | solution.py:365
  3.6 12.0 %collective-permute-start.1 = (f32[2,18,8,128]{3,2,1,0:T(8,128)}, f32[2,18,8,128]{3,2,1,0:T(8,128)S(1)}, u32[]{:S(2)}, u32[]{:S(2)}) collective-permute-start(f32[2,18,8,128]{3,2,1,0:T(8,128)} %bitcast.27), channel_id=1, source_target_pairs={{0,4},{4,8},{8,12},{12,0},{1,5},{5,9},{9,13},{13,1},{2,6},{6,10},{... | collective-permute-start | bytes 442376 | tf_op jit(solution)/shard_map/ppermute | solution.py:365
  5.2 10.4 %collective-permute-start = (f32[2,18,8,128]{3,2,1,0:T(8,128)}, f32[2,18,8,128]{3,2,1,0:T(8,128)S(1)}, u32[]{:S(2)}, u32[]{:S(2)}) collective-permute-start(f32[2,18,8,128]{3,2,1,0:T(8,128)} %bitcast.28), channel_id=1, source_target_pairs={{0,12},{4,0},{8,4},{12,8},{1,13},{5,1},{9,5},{13,9},{2,14},{6,2},{... | collective-permute-start | bytes 442376 | tf_op jit(solution)/shard_map/ppermute | solution.py:365
  7.5 2.4 %copy-start.3 = (f32[4,4,9]{2,1,0:T(4,128)S(1)}, f32[4,4,9]{2,1,0:T(4,128)}, u32[]{:S(2)}) copy-start(f32[4,4,9]{2,1,0:T(4,128)} %param.8) | copy-start | bytes 1732
  7.5 2.4 %copy-start.4 = (f32[4,4,4]{2,1,0:T(4,128)S(1)}, f32[4,4,4]{2,1,0:T(4,128)}, u32[]{:S(2)}) copy-start(f32[4,4,4]{2,1,0:T(4,128)} %constant.15) | copy-start | bytes 772
  7.5 2.4 %copy-start.5 = (f32[4,4,4]{2,1,0:T(4,128)S(1)}, f32[4,4,4]{2,1,0:T(4,128)}, u32[]{:S(2)}) copy-start(f32[4,4,4]{2,1,0:T(4,128)} %constant.14) | copy-start | bytes 772
  8.4 2.1 %copy-start.1 = (f32[1,1,2,2,3,3,4,256]{7,6,5,4,3,2,1,0:T(4,128)S(1)}, f32[1,1,2,2,3,3,4,256]{7,6,5,4,3,2,1,0:T(4,128)}, u32[]{:S(2)}) copy-start(f32[1,1,2,2,3,3,4,256]{7,6,5,4,3,2,1,0:T(4,128)} %param.7) | copy-start | bytes 442372
  8.5 2.0 %copy-start = (f32[1,1,2,2,3,3,4,256]{7,6,5,4,3,2,1,0:T(4,128)S(1)}, f32[1,1,2,2,3,3,4,256]{7,6,5,4,3,2,1,0:T(4,128)}, u32[]{:S(2)}) copy-start(f32[1,1,2,2,3,3,4,256]{7,6,5,4,3,2,1,0:T(4,128)} %param.6) | copy-start | bytes 442372
  8.5 3.8 %collective-permute-start.4 = (f32[36,128]{1,0:T(8,128)S(1)}, f32[36,128]{1,0:T(8,128)S(1)}, u32[]{:S(2)}, u32[]{:S(2)}) collective-permute-start(f32[36,128]{1,0:T(8,128)S(1)} %reshape_squeeze.7), channel_id=1, source_target_pairs={{0,2},{2,0},{1,3},{3,1},{4,6},{6,4},{5,7},{7,5},{8,10},{10,8},{9,1... | collective-permute-start | bytes 55304 | tf_op jit(solution)/shard_map/ppermute | solution.py:365
  9.8 5.8 %collective-permute-start.2 = (f32[72,128]{1,0:T(8,128)S(1)}, f32[72,128]{1,0:T(8,128)S(1)}, u32[]{:S(2)}, u32[]{:S(2)}) collective-permute-start(f32[72,128]{1,0:T(8,128)S(1)} %bitcast.33), channel_id=1, source_target_pairs={{0,4},{4,8},{8,12},{12,0},{1,5},{5,9},{9,13},{13,1},{2,6},{6,10},{... | collective-permute-start | bytes 110600 | tf_op jit(solution)/shard_map/ppermute | solution.py:365
  11.5 4.1 %copy-start.2 = (f32[1,1,2,256]{3,2,1,0:T(2,128)S(1)}, f32[1,1,2,256]{3,2,1,0:T(2,128)}, u32[]{:S(2)}) copy-start(f32[1,1,2,256]{3,2,1,0:T(2,128)} %param.9) | copy-start | bytes 6148
  18.8 1.2 %collective-permute-start.8 = (f32[4,4,9]{2,1,0:T(4,128)S(1)}, f32[4,4,9]{2,1,0:T(4,128)S(1)}, u32[]{:S(2)}, u32[]{:S(2)}) collective-permute-start(f32[4,4,9]{2,1,0:T(4,128)S(1)} %get-tuple-element.16), channel_id=1, source_target_pairs={{0,1},{1,0},{2,3},{3,2},{4,5},{5,4},{6,7},{7,6},{8,9},{9,8},{10,11... | collective-permute-start | bytes 1736 | tf_op jit(solution)/shard_map/ppermute | solution.py:382
  20.0 3.7 %collective-permute-start.9 = (f32[4,4,9]{2,1,0:T(4,128)S(1)}, f32[4,4,9]{2,1,0:T(4,128)S(1)}, u32[]{:S(2)}, u32[]{:S(2)}) collective-permute-start(f32[4,4,9]{2,1,0:T(4,128)S(1)} %add.12), channel_id=1, source_target_pairs={{0,2},{2,0},{1,3},{3,1},{4,6},{6,4},{5,7},{7,5},{8,10},{10,8},{9,1... | collective-permute-start | bytes 1736 | tf_op jit(solution)/shard_map/ppermute | solution.py:382
  23.7 3.7 %collective-permute-start.10 = (f32[4,4,9]{2,1,0:T(4,128)S(1)}, f32[4,4,9]{2,1,0:T(4,128)S(1)}, u32[]{:S(2)}, u32[]{:S(2)}) collective-permute-start(f32[4,4,9]{2,1,0:T(4,128)S(1)} %add.13), channel_id=1, source_target_pairs={{0,4},{4,0},{8,12},{12,8},{1,5},{5,1},{9,13},{13,9},{2,6},{6,2},{1... | collective-permute-start | bytes 1736 | tf_op jit(solution)/shard_map/ppermute | solution.py:382
  27.3 5.6 %collective-permute-start.11 = (f32[4,4,9]{2,1,0:T(4,128)S(1)}, f32[4,4,9]{2,1,0:T(4,128)S(1)}, u32[]{:S(2)}, u32[]{:S(2)}) collective-permute-start(f32[4,4,9]{2,1,0:T(4,128)S(1)} %add.14), channel_id=1, source_target_pairs={{0,8},{4,12},{8,0},{12,4},{1,9},{5,13},{9,1},{13,5},{2,10},{6,14},... | collective-permute-start | bytes 1736 | tf_op jit(solution)/shard_map/ppermute | solution.py:382
  27.4 6.2 %collective-permute-start.7 = (f32[2,18,8,128]{3,2,1,0:T(8,128)S(1)}, f32[2,18,8,128]{3,2,1,0:T(8,128)S(1)}, u32[]{:S(2)}, u32[]{:S(2)}) collective-permute-start(f32[2,18,8,128]{3,2,1,0:T(8,128)S(1)} %get-tuple-element.12.cot), channel_id=1, source_target_pairs={{0,2},{2,0},{1,3},{3,1},{4,6},{6,4},{5,7},{7,5},{8,10},{10,8},{9,1... | collective-permute-start | bytes 442376 | tf_op jit(solution)/shard_map/ppermute | solution.py:365
  29.1 7.1 %collective-permute-start.6 = (f32[2,18,8,128]{3,2,1,0:T(8,128)S(1)}, f32[2,18,8,128]{3,2,1,0:T(8,128)S(1)}, u32[]{:S(2)}, u32[]{:S(2)}) collective-permute-start(f32[2,18,8,128]{3,2,1,0:T(8,128)S(1)} %get-tuple-element.12.cot), channel_id=1, source_target_pairs={{0,4},{4,8},{8,12},{12,0},{1,5},{5,9},{9,13},{13,1},{2,6},{6,10},{... | collective-permute-start | bytes 442376 | tf_op jit(solution)/shard_map/ppermute | solution.py:365
  29.9 7.3 %collective-permute-start.5 = (f32[2,18,8,128]{3,2,1,0:T(8,128)S(1)}, f32[2,18,8,128]{3,2,1,0:T(8,128)S(1)}, u32[]{:S(2)}, u32[]{:S(2)}) collective-permute-start(f32[2,18,8,128]{3,2,1,0:T(8,128)S(1)} %get-tuple-element.12.cot), channel_id=1, source_target_pairs={{0,12},{4,0},{8,4},{12,8},{1,13},{5,1},{9,5},{13,9},{2,14},{6,2},{... | collective-permute-start | bytes 442376 | tf_op jit(solution)/shard_map/ppermute | solution.py:365
where the time goes:
time: 38.6 us; the launch traced here: 38.5 us
  starting transfers between devices  14.7 us (38%)
  waiting for transfers between devices  14.5 us (38%)
  Pallas kernels  5.36 us (14%)
  local copies, waits for them, and re-layouts  2.36 us (6%)
  other arithmetic  0.8 us (2%)
  between operations  0.76 us (2%)
    ppermute x8, starting transfers between devices, shifted(): lax.ppermute(value, axis, [(i, (i + offset) % count) for i in range(count)])  12.8 us
    ppermute x8, waiting for transfers between devices, shifted(): lax.ppermute(value, axis, [(i, (i + offset) % count) for i in range(count)])  7.76 us
    ppermute x4, waiting for transfers between devices, summed_over(): lax.ppermute(value, axis, [(i, i ^ step) for i in range(count)])  6.77 us
    pallas_call x4, Pallas kernels, run(): pl.pallas_call(kernel, out_shape=outs, scratch_shapes=list(scratch), comp...  5.36 us
    ppermute x4, starting transfers between devices, summed_over(): lax.ppermute(value, axis, [(i, i ^ step) for i in range(count)])  1.85 us
    slice x1, local copies, waits for them, and re-layouts, local(): z_link = gauge_links[:, :, 1, :, :, :, 1].reshape(COMPS * HALF, LANES)  0.98 us
    slice x1, local copies, waits for them, and re-layouts, local(): gauge_links[:, :, :, :, :, :, 0].reshape(PLANES * COMPS * HALF, LANES)  0.94 us
  transfers between devices with their start and end apart: 12, of which 7 were waited for; matrix products, arithmetic and copies ran while one was open for 8% of the time, Pallas kernels for 3%

commit v1 on v0

--- a/solution.py
+++ b/solution.py
@@ -1,3 +1,5 @@
+import functools
+
 import jax
 import jax.numpy as jnp
 import numpy as np
@@ -15,6 +17,8 @@
 LANES = 128
 LX = 16
 FIELD = (PLANES, COMPS, ROWS, LANES)
+MESSAGE = (PLANES * COMPS + 1, ROWS, LANES)
+TILE = (ROWS, LANES)
 F32 = jnp.float32
 
 
@@ -136,16 +140,6 @@
 def load_link(ref, plane, direction):
     index = (sublane_index() & 4) + direction
     return as_matrix([pick_rows(ref[plane, comp], index) for comp in range(COMPS)])
-
-
-def load_sent_link(ref, plane):
-    base = lax.shift_right_logical(sublane_index(), 2)
-    items = []
-    for comp in range(COMPS):
-        row = (plane * COMPS + comp) * HALF
-        start = row // ROWS * ROWS
-        items.append(pick_rows(ref[start : start + ROWS, :], base + (row - start)))
-    return as_matrix(items)
 
 
 def step_plane(value, direction, offset):
@@ -232,48 +226,95 @@
             partial[plane, comp] = sums[comp]
 
 
+def store_items(ref, plane, items):
+    for comp in range(COMPS):
+        ref[plane, comp] = items[comp]
+
+
+def store_message(ref, plane, items):
+    for comp in range(COMPS):
+        ref[plane * COMPS + comp] = items[comp]
+
+
+def load_message(ref, plane):
+    return [ref[plane * COMPS + comp] for comp in range(COMPS)]
+
+
+def pack_forward(field_in, links_in, field, links, t_send, z_send, sems):
+    copies = [
+        pltpu.make_async_copy(links_in, links, sems.at[0]),
+        pltpu.make_async_copy(field_in, field, sems.at[1]),
+    ]
+    for copy in copies:
+        copy.start()
+    for copy in copies:
+        copy.wait()
+    for plane in range(PLANES):
+        items = load_items(field, plane)
+        store_items(t_send, plane, hop_backward(load_link(links, plane, 0), items))
+        if plane == 1:
+            items = hop_backward(load_link(links, 1, 1), items)
+        store_items(z_send, plane, items)
+
+
 def far_forward(
-    links, weights, loss, partial, t_next, t_prev, t_link, z_field, z_link, out, cot, terms
+    links, weights, loss, partial, t_next, t_prev, z_near, out, cot, terms, down, up, z_send
 ):
     for plane in range(PLANES):
         sums = load_items(partial, plane)
 
-        def add(term, hop, slot):
+        def add(term, hop):
             mixed = mixed_items(weight_rows(weights, FORWARD, term), hop)
             for comp in range(COMPS):
-                terms[slot, plane, comp] = hop[comp]
                 sums[comp] = sums[comp] + mixed[comp]
 
         if plane == 0:
-            add(4, hop_backward(load_sent_link(z_link, 0), load_items(z_field, 1)), 2)
+            add(4, load_items(z_near, 1))
         else:
-            add(3, hop_forward(load_link(links, 1, 1), load_items(z_field, 0)), 2)
-        add(1, hop_forward(load_link(links, plane, 0), load_items(t_next, plane)), 0)
-        add(2, hop_backward(load_sent_link(t_link, plane), load_items(t_prev, plane)), 1)
+            hop = hop_forward(load_link(links, 1, 1), load_items(z_near, 0))
+            store_items(terms, 2, hop)
+            add(3, hop)
+        t_link = load_link(links, plane, 0)
+        hop = hop_forward(t_link, load_items(t_next, plane))
+        store_items(terms, plane, hop)
+        add(1, hop)
+        add(2, load_items(t_prev, plane))
         row = loss[plane : plane + 1, :]
         scale = jnp.where(
             sublane_index() < NCH,
             jnp.broadcast_to(row[:, :LANES], (ROWS, LANES)),
             jnp.broadcast_to(row[:, LANES:], (ROWS, LANES)),
         )
-        for comp in range(COMPS):
-            out[plane, comp] = sums[comp]
-            cot[plane, comp] = scale * sums[comp]
-
-
-def term_item(field, near, far, term, plane, comp):
+        store_items(out, plane, sums)
+        cots = [scale * item for item in sums]
+        store_items(cot, plane, cots)
+        turns = [turned(item) for item in cots]
+
+        def pulled(direction, link):
+            rows = weight_rows(weights, BACKWARD, 2 * direction + 1)
+            return hop_backward(link, [mixed_item(rows, turn) for turn in turns])
+
+        store_message(down, plane, cots)
+        store_message(up, plane, pulled(0, t_link))
+        store_items(z_send, plane, pulled(1, load_link(links, 1, 1)) if plane == 1 else cots)
+
+
+def term_item(sources, term, plane, comp):
+    field, near, far, t_prev, z_near = sources
     if term == 0:
         return field[plane, comp]
+    if term == 1:
+        return far[plane, comp]
+    if term == 2:
+        return t_prev[plane, comp]
     if term >= 5:
         return near[term - 5, plane, comp]
-    if term <= 2:
-        return far[term - 1, plane, comp]
     if (term == 3) == (plane == 0):
         return near[4, plane, comp]
-    return far[2, plane, comp]
-
-
-def weight_sums(field, cot, near, far, sums, spread):
+    return far[2, comp] if term == 3 else z_near[1, comp]
+
+
+def weight_sums(sources, cot, sums, spread):
     sub = sublane_index()
     lane = lane_index()
     for channel in range(NCH):
@@ -281,81 +322,114 @@
         for plane in range(PLANES):
             for comp in range(COMPS):
                 spread[channel, plane, comp] = pick_rows(cot[plane, comp], index)
-    rows = [jnp.zeros((ROWS, LANES), F32) for _ in range(NCH)]
+    rows = [jnp.zeros((ROWS, LANES), F32) for _ in range(2)]
     for term in range(TERMS):
         parts = [None] * NCH
         for plane in range(PLANES):
             for comp in range(COMPS):
-                value = term_item(field, near, far, term, plane, comp)
+                value = term_item(sources, term, plane, comp)
                 for channel in range(NCH):
                     piece = spread[channel, plane, comp] * value
                     parts[channel] = piece if parts[channel] is None else parts[channel] + piece
         for channel in range(NCH):
             summed = jnp.sum(parts[channel], axis=1, keepdims=True)
-            rows[channel] = jnp.where(lane == term, summed, rows[channel])
+            place = lane == (channel >> 1) * LX + term
+            rows[channel & 1] = jnp.where(place, summed, rows[channel & 1])
+    even, odd = [row + pltpu.roll(row, NCH, axis=0) for row in rows]
+    sums[...] = jnp.where(sub < NCH, even, odd)
+
+
+def store_weight_grad(ref, tile):
     for channel in range(NCH):
-        both = rows[channel] + pltpu.roll(rows[channel], NCH, axis=0)
-        sums[channel] = both[:NCH, :TERMS]
-
-
-def near_backward(field, links, weights, cot, near, far, sums, partial, spread):
-    weight_sums(field, cot, near, far, sums, spread)
-    for plane in range(PLANES):
-        turns = [turned(cot[plane, comp]) for comp in range(COMPS)]
-
-        def mixed(term):
-            rows = weight_rows(weights, BACKWARD, term)
-            return [mixed_item(rows, turn) for turn in turns]
-
-        grads = mixed(0)
+        moved = pltpu.roll(tile, LANES - LX, axis=1) if channel >> 1 else tile
+        first = (channel & 1) * NCH
+        ref[channel] = moved[first : first + NCH, :TERMS]
+
+
+def weight_partial(
+    out_in, field, cot, near, far, t_prev, z_near, sums, out, spread, sem
+):
+    copy = pltpu.make_async_copy(out_in, out, sem)
+    copy.start()
+    weight_sums((field, near, far, t_prev, z_near), cot, sums, spread)
+    copy.wait()
+
+
+def near_backward(plane, links, weights, cot, partial):
+    turns = [turned(cot[plane, comp]) for comp in range(COMPS)]
+
+    def mixed(term):
+        rows = weight_rows(weights, BACKWARD, term)
+        return [mixed_item(rows, turn) for turn in turns]
+
+    grads = mixed(0)
+
+    def add(hop):
+        for comp in range(COMPS):
+            grads[comp] = grads[comp] + hop[comp]
+
+    for direction in (2, 3):
+        link = load_link(links, plane, direction)
+        pulled = hop_backward(link, mixed(2 * direction + 1))
+        add(step_items(pulled, direction, -1))
+        add(hop_forward(link, step_items(mixed(2 * direction + 2), direction, 1)))
+    link = load_link(links, 0, 1)
+    term = 4 - plane
+    other = mixed_items(weight_rows(weights, BACKWARD, term), load_items(cot, 1 - plane))
+    add(hop_backward(link, other) if plane == 1 else hop_forward(link, other))
+    for comp in range(COMPS):
+        partial[comp] = grads[comp]
+
+
+def far_backward(count, links, weights, first, second, t_next, t_prev, z_near, *refs):
+    *sums, grad, weight_grad, held, held_sums, sems = refs
+    tiles = [ref[...] for ref in sums]
+    if len(tiles) == 2:
+        tiles += [t_prev[PLANES * COMPS], t_next[PLANES * COMPS]]
+    store_weight_grad(held_sums, paired_total(tiles) * (1.0 / count))
+    copies = [pltpu.make_async_copy(held_sums, weight_grad, sems.at[PLANES])]
+    copies[0].start()
+    for plane, partial in enumerate((first, second)):
+        grads = [partial[comp] for comp in range(COMPS)]
 
         def add(hop):
             for comp in range(COMPS):
                 grads[comp] = grads[comp] + hop[comp]
 
-        for direction in (2, 3):
-            link = load_link(links, plane, direction)
-            pulled = hop_backward(link, mixed(2 * direction + 1))
-            add(step_items(pulled, direction, -1))
-            add(hop_forward(link, step_items(mixed(2 * direction + 2), direction, 1)))
-        for comp in range(COMPS):
-            partial[plane, comp] = grads[comp]
-    link = load_link(links, 0, 1)
-    hop = hop_forward(link, mixed_items(weight_rows(weights, BACKWARD, 4), load_items(cot, 1)))
-    for comp in range(COMPS):
-        partial[0, comp] = partial[0, comp] + hop[comp]
-    hop = hop_backward(link, mixed_items(weight_rows(weights, BACKWARD, 3), load_items(cot, 0)))
-    for comp in range(COMPS):
-        partial[1, comp] = partial[1, comp] + hop[comp]
-
-
-def far_backward(links, weights, partial, t_next, t_prev, t_link, z_cot, z_link, grad):
-    for plane in range(PLANES):
-        grads = load_items(partial, plane)
-
-        def mixed(term, ref, source):
-            return mixed_items(weight_rows(weights, BACKWARD, term), load_items(ref, source))
-
-        def add(hop):
-            for comp in range(COMPS):
-                grads[comp] = grads[comp] + hop[comp]
-
-        if plane == 0:
-            add(hop_backward(load_sent_link(z_link, 0), mixed(3, z_cot, 1)))
-        else:
-            add(hop_forward(load_link(links, 1, 1), mixed(4, z_cot, 0)))
-        add(hop_forward(load_link(links, plane, 0), mixed(2, t_next, plane)))
-        add(hop_backward(load_sent_link(t_link, plane), mixed(1, t_prev, plane)))
-        for comp in range(COMPS):
-            grad[plane, comp] = grads[comp]
-
-
-def run(kernel, shapes, *operands, scratch=()):
-    outs = [jax.ShapeDtypeStruct(shape, F32) for shape in shapes]
+        def pushed(direction, term, items):
+            mixed = mixed_items(weight_rows(weights, BACKWARD, term), items)
+            return hop_forward(load_link(links, plane, direction), mixed)
+
+        add(pushed(1, 4, load_items(z_near, 0)) if plane == 1 else load_items(z_near, 1))
+        add(load_message(t_prev, plane))
+        add(pushed(0, 2, load_message(t_next, plane)))
+        store_items(held, plane, grads)
+        copies.append(pltpu.make_async_copy(held.at[plane], grad.at[plane], sems.at[plane]))
+        copies[-1].start()
+    for copy in copies:
+        copy.wait()
+
+
+def attach_sums(down_in, up_in, *refs):
+    *near_sums, down, up, sums = refs
+    tile = paired_total([ref[...] for ref in near_sums])
+    for ref in (down, up):
+        ref[PLANES * COMPS] = tile
+    sums[...] = tile
+
+
+def run(kernel, shapes, *operands, scratch=(), in_hbm=(), out_hbm=(), aliases=()):
+    def place(in_far):
+        space = pltpu.HBM if in_far else pltpu.VMEM
+        return pl.BlockSpec(memory_space=space)
+
     return pl.pallas_call(
         kernel,
-        out_shape=outs,
+        out_shape=[jax.ShapeDtypeStruct(shape, F32) for shape in shapes],
+        in_specs=[place(i in in_hbm) for i in range(len(operands))],
+        out_specs=[place(i in out_hbm) for i in range(len(shapes))],
         scratch_shapes=list(scratch),
+        input_output_aliases=dict(aliases),
         compiler_params=pltpu.CompilerParams(vmem_limit_bytes=32 * 2**20),
     )(*operands)
 
@@ -371,17 +445,29 @@
     return jnp.concatenate([shifted(block[:1], "gz", -1), shifted(block[1:], "gz", 1)], axis=0)
 
 
-def summed_over(value, axes):
+def partners(value, axes):
+    count = 1
     for axis in axes:
-        count = lax.axis_size(axis)
-        if count & (count - 1):
+        count *= lax.axis_size(axis)
+    if count == 4:
+        moved = [lax.ppermute(value, axes, [(i, i ^ k) for i in range(4)]) for k in (1, 2, 3)]
+        return [value] + moved
+    for axis in axes:
+        size = lax.axis_size(axis)
+        if size & (size - 1):
             value = lax.psum(value, axis)
             continue
         step = 1
-        while step < count:
-            value = value + lax.ppermute(value, axis, [(i, i ^ step) for i in range(count)])
+        while step < size:
+            value = value + lax.ppermute(value, axis, [(i, i ^ step) for i in range(size)])
             step *= 2
-    return value
+    return [value]
+
+
+def paired_total(values):
+    while len(values) > 1:
+        values = [a + b for a, b in zip(values[::2], values[1::2])]
+    return values[0]
 
 
 def weight_table(conv_weights):
@@ -399,61 +485,83 @@
 
 def local(gauge_links, input_field, conv_weights, loss_weight):
     shape = input_field.shape
-    field = to_rows(input_field)
-    links = to_rows(gauge_links)
-    t_link = gauge_links[:, :, :, :, :, :, 0].reshape(PLANES * COMPS * HALF, LANES)
-    z_link = gauge_links[:, :, 1, :, :, :, 1].reshape(COMPS * HALF, LANES)
-    z_field = z_planes(field)
-    t_next = shifted(field, "ta", -1)
-    t_prev = shifted(field, "ta", 1)
-    z_link = shifted(z_link, "gz", 1)
-    t_link = shifted(t_link, "ta", 1)
+    field_in = to_rows(input_field)
+    t_next = shifted(field_in, "ta", -1)
+    field, links, t_send, z_send = run(
+        pack_forward,
+        (FIELD,) * 4,
+        pltpu.with_memory_space_constraint(field_in, pltpu.HBM),
+        pltpu.with_memory_space_constraint(to_rows(gauge_links), pltpu.HBM),
+        scratch=[pltpu.SemaphoreType.DMA((2,))],
+        in_hbm=(0, 1),
+    )
+    t_prev = shifted(t_send, "ta", 1)
+    z_near = z_planes(z_send)
     weights = weight_table(conv_weights)
     loss = loss_weight.reshape(PLANES, HALF * LANES)
     partial, near = run(near_forward, (FIELD, (5,) + FIELD), field, links, weights)
-    out, cot, far = run(
+    out, cot, far, down, up, z_send = run(
         far_forward,
-        (FIELD, FIELD, (3,) + FIELD),
+        (FIELD, FIELD, (3,) + FIELD[1:], MESSAGE, MESSAGE, FIELD),
         links,
         weights,
         loss,
         partial,
         t_next,
         t_prev,
-        t_link,
-        z_field,
-        z_link,
-    )
-    z_cot = z_planes(cot)
-    t_next_cot = shifted(cot, "ta", -1)
-    t_prev_cot = shifted(cot, "ta", 1)
-    sums, grad_partial = run(
-        near_backward,
-        ((NCH, NCH, TERMS), FIELD),
+        z_near,
+    )
+    sums, out = run(
+        weight_partial,
+        (TILE, FIELD),
+        out,
         field,
-        links,
-        weights,
         cot,
         near,
         far,
-        scratch=[pltpu.VMEM((NCH,) + FIELD, F32)],
-    )
-    sums = summed_over(sums, ("rep", "gz", "ta"))
+        t_prev,
+        z_near,
+        scratch=[pltpu.VMEM((NCH,) + FIELD, F32), pltpu.SemaphoreType.DMA],
+        out_hbm=(1,),
+    )
+    down, up, sums = run(
+        attach_sums,
+        (MESSAGE, MESSAGE, TILE),
+        down,
+        up,
+        *partners(sums, ("gz", "rep")),
+        aliases=((0, 0), (1, 1)),
+    )
+    t_next_cot = shifted(down, "ta", -1)
+    t_prev_cot = shifted(up, "ta", 1)
+    z_near_cot = z_planes(z_send)
+    if lax.axis_size("ta") == 4:
+        all_sums = [sums, shifted(sums, "ta", 2)]
+    else:
+        all_sums = [paired_total(partners(sums, ("ta",)))]
+    halves = [
+        run(functools.partial(near_backward, plane), (FIELD[1:],), links, weights, cot)[0]
+        for plane in range(PLANES)
+    ]
     count = loss_weight.size
     for axis in ("ta", "gz", "rep"):
         count = count * lax.axis_size(axis)
-    weight_grad = sums / count
-    (grad,) = run(
-        far_backward,
-        (FIELD,),
+    grad, weight_grad = run(
+        functools.partial(far_backward, count),
+        (FIELD, (NCH, NCH, TERMS)),
         links,
         weights,
-        grad_partial,
+        *halves,
         t_next_cot,
         t_prev_cot,
-        t_link,
-        z_cot,
-        z_link,
+        z_near_cot,
+        *all_sums,
+        scratch=[
+            pltpu.VMEM(FIELD, F32),
+            pltpu.VMEM((NCH, NCH, TERMS), F32),
+            pltpu.SemaphoreType.DMA((PLANES + 1,)),
+        ],
+        out_hbm=(0, 1),
     )
     return from_rows(out, shape), from_rows(grad, shape), weight_grad
 

time: 38.6 us -> 30.2 us (0.78)
  waiting for transfers between devices: 14.5 us -> 10.2 us
  local copies, waits for them, and re-layouts: 2.36 us -> 0.41 us
  starting transfers between devices: 14.7 us -> 13 us
  other arithmetic: 0.8 us -> 0.19 us
    ppermute x4 -> x3, waiting for transfers between devices: 6.77 us -> 1.83 us  [partners(): lax.ppermute(value, axes, [(i, i ^ k) for i in range(4)])]
    slice x2 -> x0, local copies, waits for them, and re-layouts: 1.92 us -> none  [the longest x1 0.98 us: local(): z_link = gauge_links[:, :, 1, :, :, :, 1].reshape(COMPS * HALF, LANES)]
    ppermute x8 -> x7, starting transfers between devices: 12.8 us -> 11.1 us  [shifted(): lax.ppermute(value, axis, [(i, (i + offset) % count) for i in range(count)])]
    ppermute x8 -> x7, waiting for transfers between devices: 7.76 us -> 8.4 us  [shifted(): lax.ppermute(value, axis, [(i, (i + offset) % count) for i in range(count)])]
    div x1 -> x0, other arithmetic: 0.6 us -> none  [local(): weight_grad = sums / count]
    pallas_call x4 -> x8, Pallas kernels: 5.36 us -> 5.54 us  [run(): pl.pallas_call(kernel, out_shape=[jax.ShapeDtypeStruct(shape, F32) for sh...]
    ppermute x4 -> x3, starting transfers between devices: 1.85 us -> 1.92 us  [partners(): lax.ppermute(value, axes, [(i, i ^ k) for i in range(4)])]
  transfers between devices with their start and end apart: 12 -> 10, of which waited for: 7 -> 6; matrix products, arithmetic and copies ran while one was open for 8% -> 2% of each run, Pallas kernels for 3% -> 11%
where the time goes in v1:
time: 30.2 us; the launch traced here: 30.1 us
  starting transfers between devices  13 us (43%)
  waiting for transfers between devices  10.2 us (34%)
  Pallas kernels  5.54 us (18%)
  between operations  0.72 us (2%)
  local copies, waits for them, and re-layouts  0.41 us (1%)
    ppermute x7, starting transfers between devices, shifted(): lax.ppermute(value, axis, [(i, (i + offset) % count) for i in range(count)])  11.1 us
    ppermute x7, waiting for transfers between devices, shifted(): lax.ppermute(value, axis, [(i, (i + offset) % count) for i in range(count)])  8.4 us
    pallas_call x8, Pallas kernels, run(): pl.pallas_call(kernel, out_shape=[jax.ShapeDtypeStruct(shape, F32) for sh...  5.54 us
    ppermute x3, starting transfers between devices, partners(): lax.ppermute(value, axes, [(i, i ^ k) for i in range(4)])  1.92 us
    ppermute x3, waiting for transfers between devices, partners(): lax.ppermute(value, axes, [(i, i ^ k) for i in range(4)])  1.83 us
  transfers between devices with their start and end apart: 10, of which 6 were waited for; matrix products, arithmetic and copies ran while one was open for 2% of the time, Pallas kernels for 11%

profile of v1, /device:TPU:0, one launch (start us, length us, event | category | flops | bytes accessed | tf_op | source)
XLA Modules:
  0.0 30.1 jit_solution(14621373900599916788)
XLA Ops:
  0.6 5.1 %collective-permute-start = (f32[2,18,8,128]{3,2,1,0:T(8,128)}, f32[2,18,8,128]{3,2,1,0:T(8,128)S(1)}, u32[]{:S(2)}, u32[]{:S(2)}) collective-permute-start(f32[2,18,8,128]{3,2,1,0:T(8,128)} %bitcast.23), channel_id=1, source_target_pairs={{0,12},{4,0},{8,4},{12,8},{1,13},{5,1},{9,5},{13,9},{2,14},{6,2},{... | collective-permute-start | bytes 442376 | tf_op jit(solution)/shard_map/ppermute | solution.py:439
  5.7 0.0 copy-start.1
  5.7 0.0 copy-start.2
  5.7 0.0 copy-start.3
  5.7 1.2 %shard_map.85 = (f32[2,18,8,128]{3,2,1,0:T(8,128)S(1)}, f32[2,18,8,128]{3,2,1,0:T(8,128)S(1)}, f32[2,18,8,128]{3,2,1,0:T(8,128)S(1)}, f32[2,18,8,128]{3,2,1,0:T(8,128)S(1)}) custom-call(f32[2,18,8,128]{3,2,1,0:T(8,128)} %bitcast.24, f32[2,18,8,128]{3,2,1,0:T(8,128)} %bitcast.22), custom_call_target="tpu_custom_call" | custom-call | tf_op jit(solution)/shard_map/pallas_call | solution.py:426
  7.0 0.1 collective-permute-start.1
  7.0 1.6 %collective-permute-start.2 = (f32[2,18,8,128]{3,2,1,0:T(8,128)S(1)}, f32[2,18,8,128]{3,2,1,0:T(8,128)S(1)}, u32[]{:S(2)}, u32[]{:S(2)}) collective-permute-start(f32[2,18,8,128]{3,2,1,0:T(8,128)S(1)} %get-tuple-element.26), channel_id=1, source_target_pairs={{0,2},{2,0},{1,3},{3,1},{4,6},{6,4},{5,7},{7,5},{8,10},{10,8},{9,1... | collective-permute-start | bytes 442376 | tf_op jit(solution)/shard_map/ppermute | solution.py:439
  8.6 0.0 copy-done.1
  8.6 0.0 copy-done.2
  8.6 0.0 copy-done.3
  8.6 0.1 multiply_reduce_fusion.1
  8.7 0.1 copy.21
  8.8 0.1 reshape.44
  8.9 0.1 copy.22
  9.0 0.1 reshape.45
  9.1 0.1 maximum_maximum_fusion.weights
  9.2 1.0 %shard_map.86 = (f32[2,18,8,128]{3,2,1,0:T(8,128)S(1)}, f32[5,2,18,8,128]{4,3,2,1,0:T(8,128)S(1)}) custom-call(f32[2,18,8,128]{3,2,1,0:T(8,128)S(1)} %get-tuple-element.23.field, f32[2,18,8,128]{3,2,1,0:T(8,128)S(1)} %get-tuple-element.22.links, f32[8,72]{1,0:T(8,128)S(1)} %maximum_maximum_fusion.weights), custom_call_target="tpu_custom_call" | custom-call | tf_op jit(solution)/shard_map/pallas_call | solution.py:426
  10.2 0.0 copy-start
  10.2 0.1 collective-permute-done.t_next
  10.3 3.8 %collective-permute-done.1.t_prev = f32[2,18,8,128]{3,2,1,0:T(8,128)S(1)} collective-permute-done((f32[2,18,8,128]{3,2,1,0:T(8,128)S(1)}, f32[2,18,8,128]{3,2,1,0:T(8,128)S(1)}, u32[]{:S(2)}, u32[]{:S(2)}) %collective-permute-start.1) | collective-permute-done | bytes 147488 | tf_op jit(solution)/shard_map/ppermute | solution.py:439
  14.1 0.0 collective-permute-done.2.z_near
  14.1 0.0 copy-done
  14.1 0.6 %shard_map.87 = (f32[2,18,8,128]{3,2,1,0:T(8,128)S(1)}, f32[2,18,8,128]{3,2,1,0:T(8,128)S(1)}, f32[3,18,8,128]{3,2,1,0:T(8,128)S(1)}, f32[37,8,128]{2,1,0:T(8,12...) custom-call(f32[2,18,8,128]{3,2,1,0:T(8,128)S(1)} %get-tuple-element.22.links, ...), custom_call_target="tpu_custom_call" | custom-call | tf_op jit(solution)/shard_map/pallas_call | solution.py:426
  14.8 0.7 %shard_map.88 = (f32[8,128]{1,0:T(8,128)S(1)}, f32[2,18,8,128]{3,2,1,0:T(8,128)}) custom-call(f32[2,18,8,128]{3,2,1,0:T(8,128)S(1)} %get-tuple-element.27.out_in, f32[2,18,8,128]{3,2,1,0:T(8,128)S(1)} %get-tuple-element.23.field, f32[2,18,8,128]{3,2,1,0:T(8,128)S(1)} %get-tuple-element.28.cot, f32[5,2,18,8,128]{4,3,2,1,0:T(8,128)S(1)} %get-tuple-element.29.near, ...), custom_call_target="tpu_custom_call" | custom-call | tf_op jit(solution)/shard_map/pallas_call | solution.py:426
  15.4 0.1 collective-permute-start.5
  15.5 1.6 %collective-permute-start.4 = (f32[8,128]{1,0:T(8,128)S(1)}, f32[8,128]{1,0:T(8,128)S(1)}, u32[]{:S(2)}, u32[]{:S(2)}) collective-permute-start(f32[8,128]{1,0:T(8,128)S(1)} %get-tuple-element.34.refs_0_), channel_id=1, source_target_pairs={{0,2},{1,3},{2,0},{3,1},{4,6},{5,7},{6,4},{7,5},{8,10},{9,11},{10,... | collective-permute-start | bytes 12296 | tf_op jit(solution)/shard_map/ppermute | solution.py:453
  17.1 0.3 collective-permute-start.3
  17.4 1.2 %collective-permute-done.5.refs_3_ = f32[8,128]{1,0:T(8,128)S(1)} collective-permute-done((f32[8,128]{1,0:T(8,128)S(1)}, f32[8,128]{1,0:T(8,128)S(1)}, u32[]{:S(2)}, u32[]{:S(2)}) %collective-permute-start.5) | collective-permute-done | bytes 4128 | tf_op jit(solution)/shard_map/ppermute | solution.py:453
  18.5 0.7 %collective-permute-done.4.refs_2_ = f32[8,128]{1,0:T(8,128)S(1)} collective-permute-done((f32[8,128]{1,0:T(8,128)S(1)}, f32[8,128]{1,0:T(8,128)S(1)}, u32[]{:S(2)}, u32[]{:S(2)}) %collective-permute-start.4) | collective-permute-done | bytes 4128 | tf_op jit(solution)/shard_map/ppermute | solution.py:453
  19.2 0.0 collective-permute-done.3.refs_1_
  19.2 2.2 %collective-permute-start.6 = (f32[37,8,128]{2,1,0:T(8,128)S(1)}, f32[37,8,128]{2,1,0:T(8,128)S(1)}, u32[]{:S(2)}, u32[]{:S(2)}) collective-permute-start(f32[37,8,128]{2,1,0:T(8,128)S(1)} %get-tuple-element.35), channel_id=1, source_target_pairs={{0,12},{4,0},{8,4},{12,8},{1,13},{5,1},{9,5},{13,9},{2,14},{6,2},{... | collective-permute-start | bytes 454664 | tf_op jit(solution)/shard_map/ppermute | solution.py:439
  21.4 0.0 collective-permute-start.7
  21.4 1.3 %collective-permute-start.8 = (f32[2,18,8,128]{3,2,1,0:T(8,128)S(1)}, f32[2,18,8,128]{3,2,1,0:T(8,128)S(1)}, u32[]{:S(2)}, u32[]{:S(2)}) collective-permute-start(f32[2,18,8,128]{3,2,1,0:T(8,128)S(1)} %get-tuple-element.37), channel_id=1, source_target_pairs={{0,2},{2,0},{1,3},{3,1},{4,6},{6,4},{5,7},{7,5},{8,10},{10,8},{9,1... | collective-permute-start | bytes 442376 | tf_op jit(solution)/shard_map/ppermute | solution.py:439
  22.8 0.8 %collective-permute-start.9 = (f32[8,128]{1,0:T(8,128)S(1)}, f32[8,128]{1,0:T(8,128)S(1)}, u32[]{:S(2)}, u32[]{:S(2)}) collective-permute-start(f32[8,128]{1,0:T(8,128)S(1)} %get-tuple-element.38.refs_0_), channel_id=1, source_target_pairs={{0,8},{4,12},{8,0},{12,4},{1,9},{5,13},{9,1},{13,5},{2,10},{6,14},... | collective-permute-start | bytes 12296 | tf_op jit(solution)/shard_map/ppermute | solution.py:439
  23.6 0.5 %shard_map.90.second = f32[18,8,128]{2,1,0:T(8,128)S(1)} custom-call(f32[2,18,8,128]{3,2,1,0:T(8,128)S(1)} %get-tuple-element.22.links, f32[8,72]{1,0:T(8,128)S(1)} %maximum_maximum_fusion.weights, f32[2,18,8,128]{3,2,1,0:T(8,128)S(1)} %get-tuple-element.28.cot), custom_call_target="tpu_custom_call" | custom-call | tf_op jit(solution)/shard_map/pallas_call | solution.py:426
  24.1 0.5 %shard_map.89.first = f32[18,8,128]{2,1,0:T(8,128)S(1)} custom-call(f32[2,18,8,128]{3,2,1,0:T(8,128)S(1)} %get-tuple-element.22.links, f32[8,72]{1,0:T(8,128)S(1)} %maximum_maximum_fusion.weights, f32[2,18,8,128]{3,2,1,0:T(8,128)S(1)} %get-tuple-element.28.cot), custom_call_target="tpu_custom_call" | custom-call | tf_op jit(solution)/shard_map/pallas_call | solution.py:426
  24.6 3.7 %collective-permute-done.9.refs_1_ = f32[8,128]{1,0:T(8,128)S(1)} collective-permute-done((f32[8,128]{1,0:T(8,128)S(1)}, f32[8,128]{1,0:T(8,128)S(1)}, u32[]{:S(2)}, u32[]{:S(2)}) %collective-permute-start.9) | collective-permute-done | bytes 4128 | tf_op jit(solution)/shard_map/ppermute | solution.py:439
  28.3 0.0 collective-permute-done.8.z_near
  28.3 0.0 collective-permute-done.6.t_next
  28.3 0.8 %collective-permute-done.7.t_prev = f32[37,8,128]{2,1,0:T(8,128)S(1)} collective-permute-done((f32[37,8,128]{2,1,0:T(8,128)S(1)}, f32[37,8,128]{2,1,0:T(8,128)S(1)}, u32[]{:S(2)}, u32[]{:S(2)}) %collective-permute-start.7) | collective-permute-done | bytes 151584 | tf_op jit(solution)/shard_map/ppermute | solution.py:439
  29.1 1.0 %shard_map.92 = (f32[2,18,8,128]{3,2,1,0:T(8,128)}, f32[4,4,9]{2,1,0:T(4,128)}) custom-call(f32[2,18,8,128]{3,2,1,0:T(8,128)S(1)} %get-tuple-element.22.links, f32[8,72]{1,0:T(8,128)S(1)} %maximum_maximum_fusion.weights, f32[18,8,128]{2,1,0:T(8,128)S(1)} %shard_map.89.first, f32[18,8,128]{2,1,0:T(8,128)S(1)} %shard_map.90.second, ...), custom_call_target="tpu_custom_call" | custom-call | tf_op jit(solution)/shard_map/pallas_call | solution.py:426
  (1 shorter events, 0.0 us)
Async XLA Ops:
  0.6 9.7 %collective-permute-start = (f32[2,18,8,128]{3,2,1,0:T(8,128)}, f32[2,18,8,128]{3,2,1,0:T(8,128)S(1)}, u32[]{:S(2)}, u32[]{:S(2)}) collective-permute-start(f32[2,18,8,128]{3,2,1,0:T(8,128)} %bitcast.23), channel_id=1, source_target_pairs={{0,12},{4,0},{8,4},{12,8},{1,13},{5,1},{9,5},{13,9},{2,14},{6,2},{... | collective-permute-start | bytes 442376 | tf_op jit(solution)/shard_map/ppermute | solution.py:439
  5.7 2.9 %copy-start.1 = (f32[4,4,9]{2,1,0:T(4,128)S(1)}, f32[4,4,9]{2,1,0:T(4,128)}, u32[]{:S(2)}) copy-start(f32[4,4,9]{2,1,0:T(4,128)} %param.8) | copy-start | bytes 1732
  5.7 2.9 %copy-start.2 = (f32[4,4,4]{2,1,0:T(4,128)S(1)}, f32[4,4,4]{2,1,0:T(4,128)}, u32[]{:S(2)}) copy-start(f32[4,4,4]{2,1,0:T(4,128)} %constant.12) | copy-start | bytes 772
  5.7 2.9 %copy-start.3 = (f32[4,4,4]{2,1,0:T(4,128)S(1)}, f32[4,4,4]{2,1,0:T(4,128)}, u32[]{:S(2)}) copy-start(f32[4,4,4]{2,1,0:T(4,128)} %constant.11) | copy-start | bytes 772
  7.0 7.2 %collective-permute-start.1 = (f32[2,18,8,128]{3,2,1,0:T(8,128)S(1)}, f32[2,18,8,128]{3,2,1,0:T(8,128)S(1)}, u32[]{:S(2)}, u32[]{:S(2)}) collective-permute-start(f32[2,18,8,128]{3,2,1,0:T(8,128)S(1)} %get-tuple-element.25), channel_id=1, source_target_pairs={{0,4},{4,8},{8,12},{12,0},{1,5},{5,9},{9,13},{13,1},{2,6},{6,10},{... | collective-permute-start | bytes 442376 | tf_op jit(solution)/shard_map/ppermute | solution.py:439
  7.0 7.1 %collective-permute-start.2 = (f32[2,18,8,128]{3,2,1,0:T(8,128)S(1)}, f32[2,18,8,128]{3,2,1,0:T(8,128)S(1)}, u32[]{:S(2)}, u32[]{:S(2)}) collective-permute-start(f32[2,18,8,128]{3,2,1,0:T(8,128)S(1)} %get-tuple-element.26), channel_id=1, source_target_pairs={{0,2},{2,0},{1,3},{3,1},{4,6},{6,4},{5,7},{7,5},{8,10},{10,8},{9,1... | collective-permute-start | bytes 442376 | tf_op jit(solution)/shard_map/ppermute | solution.py:439
  10.2 3.9 %copy-start = (f32[1,1,2,256]{3,2,1,0:T(2,128)S(1)}, f32[1,1,2,256]{3,2,1,0:T(2,128)}, u32[]{:S(2)}) copy-start(f32[1,1,2,256]{3,2,1,0:T(2,128)} %param.9) | copy-start | bytes 6148
  15.4 3.1 %collective-permute-start.5 = (f32[8,128]{1,0:T(8,128)S(1)}, f32[8,128]{1,0:T(8,128)S(1)}, u32[]{:S(2)}, u32[]{:S(2)}) collective-permute-start(f32[8,128]{1,0:T(8,128)S(1)} %get-tuple-element.34.refs_0_), channel_id=1, source_target_pairs={{0,3},{1,2},{2,1},{3,0},{4,7},{5,6},{6,5},{7,4},{8,11},{9,10},{10,... | collective-permute-start | bytes 12296 | tf_op jit(solution)/shard_map/ppermute | solution.py:453
  15.5 3.7 %collective-permute-start.4 = (f32[8,128]{1,0:T(8,128)S(1)}, f32[8,128]{1,0:T(8,128)S(1)}, u32[]{:S(2)}, u32[]{:S(2)}) collective-permute-start(f32[8,128]{1,0:T(8,128)S(1)} %get-tuple-element.34.refs_0_), channel_id=1, source_target_pairs={{0,2},{1,3},{2,0},{3,1},{4,6},{5,7},{6,4},{7,5},{8,10},{9,11},{10,... | collective-permute-start | bytes 12296 | tf_op jit(solution)/shard_map/ppermute | solution.py:453
  17.1 2.1 %collective-permute-start.3 = (f32[8,128]{1,0:T(8,128)S(1)}, f32[8,128]{1,0:T(8,128)S(1)}, u32[]{:S(2)}, u32[]{:S(2)}) collective-permute-start(f32[8,128]{1,0:T(8,128)S(1)} %get-tuple-element.34.refs_0_), channel_id=1, source_target_pairs={{0,1},{1,0},{2,3},{3,2},{4,5},{5,4},{6,7},{7,6},{8,9},{9,8},{10,11... | collective-permute-start | bytes 12296 | tf_op jit(solution)/shard_map/ppermute | solution.py:453
  19.2 9.1 %collective-permute-start.6 = (f32[37,8,128]{2,1,0:T(8,128)S(1)}, f32[37,8,128]{2,1,0:T(8,128)S(1)}, u32[]{:S(2)}, u32[]{:S(2)}) collective-permute-start(f32[37,8,128]{2,1,0:T(8,128)S(1)} %get-tuple-element.35), channel_id=1, source_target_pairs={{0,12},{4,0},{8,4},{12,8},{1,13},{5,1},{9,5},{13,9},{2,14},{6,2},{... | collective-permute-start | bytes 454664 | tf_op jit(solution)/shard_map/ppermute | solution.py:439
  21.4 7.7 %collective-permute-start.7 = (f32[37,8,128]{2,1,0:T(8,128)S(1)}, f32[37,8,128]{2,1,0:T(8,128)S(1)}, u32[]{:S(2)}, u32[]{:S(2)}) collective-permute-start(f32[37,8,128]{2,1,0:T(8,128)S(1)} %get-tuple-element.36), channel_id=1, source_target_pairs={{0,4},{4,8},{8,12},{12,0},{1,5},{5,9},{9,13},{13,1},{2,6},{6,10},{... | collective-permute-start | bytes 454664 | tf_op jit(solution)/shard_map/ppermute | solution.py:439
  21.4 6.9 %collective-permute-start.8 = (f32[2,18,8,128]{3,2,1,0:T(8,128)S(1)}, f32[2,18,8,128]{3,2,1,0:T(8,128)S(1)}, u32[]{:S(2)}, u32[]{:S(2)}) collective-permute-start(f32[2,18,8,128]{3,2,1,0:T(8,128)S(1)} %get-tuple-element.37), channel_id=1, source_target_pairs={{0,2},{2,0},{1,3},{3,1},{4,6},{6,4},{5,7},{7,5},{8,10},{10,8},{9,1... | collective-permute-start | bytes 442376 | tf_op jit(solution)/shard_map/ppermute | solution.py:439
  22.8 5.5 %collective-permute-start.9 = (f32[8,128]{1,0:T(8,128)S(1)}, f32[8,128]{1,0:T(8,128)S(1)}, u32[]{:S(2)}, u32[]{:S(2)}) collective-permute-start(f32[8,128]{1,0:T(8,128)S(1)} %get-tuple-element.38.refs_0_), channel_id=1, source_target_pairs={{0,8},{4,12},{8,0},{12,4},{1,9},{5,13},{9,1},{13,5},{2,10},{6,14},... | collective-permute-start | bytes 12296 | tf_op jit(solution)/shard_map/ppermute | solution.py:439

commit v2 on v1

--- a/solution.py
+++ b/solution.py
@@ -347,11 +347,14 @@
 
 
 def weight_partial(
-    out_in, field, cot, near, far, t_prev, z_near, sums, out, spread, sem
+    out_in, field, cot, near, far, t_prev, z_near, *refs
 ):
+    down, up, sums, out, spread, sem = refs[2:]
     copy = pltpu.make_async_copy(out_in, out, sem)
     copy.start()
     weight_sums((field, near, far, t_prev, z_near), cot, sums, spread)
+    for ref in (down, up):
+        ref[PLANES * COMPS] = sums[...]
     copy.wait()
 
 
@@ -381,14 +384,8 @@
         partial[comp] = grads[comp]
 
 
-def far_backward(count, links, weights, first, second, t_next, t_prev, z_near, *refs):
-    *sums, grad, weight_grad, held, held_sums, sems = refs
-    tiles = [ref[...] for ref in sums]
-    if len(tiles) == 2:
-        tiles += [t_prev[PLANES * COMPS], t_next[PLANES * COMPS]]
-    store_weight_grad(held_sums, paired_total(tiles) * (1.0 / count))
-    copies = [pltpu.make_async_copy(held_sums, weight_grad, sems.at[PLANES])]
-    copies[0].start()
+def far_backward(links, weights, first, second, t_next, t_prev, z_near, grad, held, sems):
+    copies = []
     for plane, partial in enumerate((first, second)):
         grads = [partial[comp] for comp in range(COMPS)]
 
@@ -410,12 +407,14 @@
         copy.wait()
 
 
-def attach_sums(down_in, up_in, *refs):
-    *near_sums, down, up, sums = refs
-    tile = paired_total([ref[...] for ref in near_sums])
-    for ref in (down, up):
-        ref[PLANES * COMPS] = tile
-    sums[...] = tile
+def line_sums(own, opposite, t_next, t_prev, sums):
+    last = PLANES * COMPS
+    sums[...] = (own[...] + opposite[...]) + (t_prev[last] + t_next[last])
+
+
+def all_sums(count, *refs):
+    tile = paired_total([ref[...] for ref in refs[:-1]])
+    store_weight_grad(refs[-1], tile * (1.0 / count))
 
 
 def run(kernel, shapes, *operands, scratch=(), in_hbm=(), out_hbm=(), aliases=()):
@@ -511,9 +510,9 @@
         t_prev,
         z_near,
     )
-    sums, out = run(
+    down, up, sums, out = run(
         weight_partial,
-        (TILE, FIELD),
+        (MESSAGE, MESSAGE, TILE, FIELD),
         out,
         field,
         cot,
@@ -521,47 +520,45 @@
         far,
         t_prev,
         z_near,
-        scratch=[pltpu.VMEM((NCH,) + FIELD, F32), pltpu.SemaphoreType.DMA],
-        out_hbm=(1,),
-    )
-    down, up, sums = run(
-        attach_sums,
-        (MESSAGE, MESSAGE, TILE),
         down,
         up,
-        *partners(sums, ("gz", "rep")),
-        aliases=((0, 0), (1, 1)),
+        scratch=[pltpu.VMEM((NCH,) + FIELD, F32), pltpu.SemaphoreType.DMA],
+        out_hbm=(3,),
+        aliases=((7, 0), (8, 1)),
     )
     t_next_cot = shifted(down, "ta", -1)
     t_prev_cot = shifted(up, "ta", 1)
     z_near_cot = z_planes(z_send)
     if lax.axis_size("ta") == 4:
-        all_sums = [sums, shifted(sums, "ta", 2)]
+        opposite = shifted(sums, "ta", 2)
     else:
-        all_sums = [paired_total(partners(sums, ("ta",)))]
+        sums = paired_total(partners(sums, ("ta",)))
     halves = [
         run(functools.partial(near_backward, plane), (FIELD[1:],), links, weights, cot)[0]
         for plane in range(PLANES)
     ]
+    sums, *halves = lax.optimization_barrier((sums, *halves))
+    if lax.axis_size("ta") == 4:
+        (sums,) = run(line_sums, (TILE,), sums, opposite, t_next_cot, t_prev_cot)
     count = loss_weight.size
     for axis in ("ta", "gz", "rep"):
         count = count * lax.axis_size(axis)
-    grad, weight_grad = run(
-        functools.partial(far_backward, count),
-        (FIELD, (NCH, NCH, TERMS)),
+    (weight_grad,) = run(
+        functools.partial(all_sums, count),
+        ((NCH, NCH, TERMS),),
+        *partners(sums, ("gz", "rep")),
+    )
+    (grad,) = run(
+        far_backward,
+        (FIELD,),
         links,
         weights,
         *halves,
         t_next_cot,
         t_prev_cot,
         z_near_cot,
-        *all_sums,
-        scratch=[
-            pltpu.VMEM(FIELD, F32),
-            pltpu.VMEM((NCH, NCH, TERMS), F32),
-            pltpu.SemaphoreType.DMA((PLANES + 1,)),
-        ],
-        out_hbm=(0, 1),
+        scratch=[pltpu.VMEM(FIELD, F32), pltpu.SemaphoreType.DMA((PLANES,))],
+        out_hbm=(0,),
     )
     return from_rows(out, shape), from_rows(grad, shape), weight_grad
 

time: 30.2 us -> 28.9 us (0.957)
  waiting for transfers between devices: 10.2 us -> 8.29 us
  Pallas kernels: 5.54 us -> 6.19 us
    ppermute x3, waiting for transfers between devices: 1.83 us -> 0.83 us  [partners(): lax.ppermute(value, axes, [(i, i ^ k) for i in range(4)])]
    ppermute x7, waiting for transfers between devices: 8.4 us -> 7.46 us  [shifted(): lax.ppermute(value, axis, [(i, (i + offset) % count) for i in range(count)])]
    pallas_call x8 -> x9, Pallas kernels: 5.54 us -> 6.19 us  [run(): pl.pallas_call(kernel, out_shape=[jax.ShapeDtypeStruct(shape, F32) for sh...]
  transfers between devices with their start and end apart: 10 -> 10, of which waited for: 6 -> 6; matrix products, arithmetic and copies ran while one was open for 2% -> 2% of each run, Pallas kernels for 11% -> 15%
where the time goes in v2:
time: 28.9 us; the launch traced here: 28.7 us
  starting transfers between devices  12.9 us (45%)
  waiting for transfers between devices  8.29 us (29%)
  Pallas kernels  6.19 us (21%)
  between operations  0.72 us (2%)
  local copies, waits for them, and re-layouts  0.41 us (1%)
    ppermute x7, starting transfers between devices, shifted(): lax.ppermute(value, axis, [(i, (i + offset) % count) for i in range(count)])  11.1 us
    ppermute x7, waiting for transfers between devices, shifted(): lax.ppermute(value, axis, [(i, (i + offset) % count) for i in range(count)])  7.46 us
    pallas_call x9, Pallas kernels, run(): pl.pallas_call(kernel, out_shape=[jax.ShapeDtypeStruct(shape, F32) for sh...  6.19 us
    ppermute x3, starting transfers between devices, partners(): lax.ppermute(value, axes, [(i, i ^ k) for i in range(4)])  1.86 us
    ppermute x3, waiting for transfers between devices, partners(): lax.ppermute(value, axes, [(i, i ^ k) for i in range(4)])  0.83 us
  transfers between devices with their start and end apart: 10, of which 6 were waited for; matrix products, arithmetic and copies ran while one was open for 2% of the time, Pallas kernels for 15%

profile of v2, /device:TPU:0, one launch (start us, length us, event | category | flops | bytes accessed | tf_op | source)
XLA Modules:
  0.0 28.7 jit_solution(993942132909344382)
XLA Ops:
  0.6 5.1 %collective-permute-start = (f32[2,18,8,128]{3,2,1,0:T(8,128)}, f32[2,18,8,128]{3,2,1,0:T(8,128)S(1)}, u32[]{:S(2)}, u32[]{:S(2)}) collective-permute-start(f32[2,18,8,128]{3,2,1,0:T(8,128)} %bitcast.24), channel_id=1, source_target_pairs={{0,12},{4,0},{8,4},{12,8},{1,13},{5,1},{9,5},{13,9},{2,14},{6,2},{... | collective-permute-start | bytes 442376 | tf_op jit(solution)/shard_map/ppermute | solution.py:438
  5.7 0.0 copy-start.1
  5.7 0.0 copy-start.2
  5.7 0.0 copy-start.3
  5.7 1.2 %shard_map.85 = (f32[2,18,8,128]{3,2,1,0:T(8,128)S(1)}, f32[2,18,8,128]{3,2,1,0:T(8,128)S(1)}, f32[2,18,8,128]{3,2,1,0:T(8,128)S(1)}, f32[2,18,8,128]{3,2,1,0:T(8,128)S(1)}) custom-call(f32[2,18,8,128]{3,2,1,0:T(8,128)} %bitcast.25, f32[2,18,8,128]{3,2,1,0:T(8,128)} %bitcast.23), custom_call_target="tpu_custom_call" | custom-call | tf_op jit(solution)/shard_map/pallas_call | solution.py:425
  7.0 0.1 collective-permute-start.1
  7.0 1.6 %collective-permute-start.2 = (f32[2,18,8,128]{3,2,1,0:T(8,128)S(1)}, f32[2,18,8,128]{3,2,1,0:T(8,128)S(1)}, u32[]{:S(2)}, u32[]{:S(2)}) collective-permute-start(f32[2,18,8,128]{3,2,1,0:T(8,128)S(1)} %get-tuple-element.26), channel_id=1, source_target_pairs={{0,2},{2,0},{1,3},{3,1},{4,6},{6,4},{5,7},{7,5},{8,10},{10,8},{9,1... | collective-permute-start | bytes 442376 | tf_op jit(solution)/shard_map/ppermute | solution.py:438
  8.6 0.0 copy-done.1
  8.6 0.0 copy-done.2
  8.6 0.0 copy-done.3
  8.6 0.1 multiply_reduce_fusion.1
  8.7 0.1 copy.21
  8.8 0.1 reshape.44
  8.9 0.1 copy.22
  9.0 0.1 reshape.45
  9.1 0.1 maximum_maximum_fusion.weights
  9.2 1.0 %shard_map.86 = (f32[2,18,8,128]{3,2,1,0:T(8,128)S(1)}, f32[5,2,18,8,128]{4,3,2,1,0:T(8,128)S(1)}) custom-call(f32[2,18,8,128]{3,2,1,0:T(8,128)S(1)} %get-tuple-element.23.field, f32[2,18,8,128]{3,2,1,0:T(8,128)S(1)} %get-tuple-element.22.links, f32[8,72]{1,0:T(8,128)S(1)} %maximum_maximum_fusion.weights), custom_call_target="tpu_custom_call" | custom-call | tf_op jit(solution)/shard_map/pallas_call | solution.py:425
  10.2 0.0 copy-start
  10.2 0.1 collective-permute-done.t_next
  10.3 3.8 %collective-permute-done.1.t_prev = f32[2,18,8,128]{3,2,1,0:T(8,128)S(1)} collective-permute-done((f32[2,18,8,128]{3,2,1,0:T(8,128)S(1)}, f32[2,18,8,128]{3,2,1,0:T(8,128)S(1)}, u32[]{:S(2)}, u32[]{:S(2)}) %collective-permute-start.1) | collective-permute-done | bytes 147488 | tf_op jit(solution)/shard_map/ppermute | solution.py:438
  14.1 0.0 collective-permute-done.2.z_near
  14.1 0.0 copy-done
  14.1 0.6 %shard_map.87 = (f32[2,18,8,128]{3,2,1,0:T(8,128)S(1)}, f32[2,18,8,128]{3,2,1,0:T(8,128)S(1)}, f32[3,18,8,128]{3,2,1,0:T(8,128)S(1)}, f32[37,8,128]{2,1,0:T(8,12...) custom-call(f32[2,18,8,128]{3,2,1,0:T(8,128)S(1)} %get-tuple-element.22.links, ...), custom_call_target="tpu_custom_call" | custom-call | tf_op jit(solution)/shard_map/pallas_call | solution.py:425
  14.8 0.7 %shard_map.88 = (f32[37,8,128]{2,1,0:T(8,128)S(1)}, f32[37,8,128]{2,1,0:T(8,128)S(1)}, f32[8,128]{1,0:T(8,128)S(1)}, f32[2,18,8,128]{3,2,1,0:T(8,128)}) custom-call(f32[2,18,8,128]{3,2,1,0:T(8,128)S(1)} %get-tuple-element.27.out_in, f32[2,18,8,128]{3,2,1,0:T(8,128)S(1)} %get-tuple-element.23.field, ...), custom_call_target="tpu_custom_call", output_to_operand_aliasing={{0}: (7, {}), {1}: (8, {})} | custom-call | tf_op jit(solution)/shard_map/pallas_call | solution.py:425
  15.4 1.9 %collective-permute-start.3 = (f32[37,8,128]{2,1,0:T(8,128)S(1)}, f32[37,8,128]{2,1,0:T(8,128)S(1)}, u32[]{:S(2)}, u32[]{:S(2)}) collective-permute-start(f32[37,8,128]{2,1,0:T(8,128)S(1)} %get-tuple-element.37), channel_id=1, source_target_pairs={{0,12},{4,0},{8,4},{12,8},{1,13},{5,1},{9,5},{13,9},{2,14},{6,2},{... | collective-permute-start | bytes 454664 | tf_op jit(solution)/shard_map/ppermute | solution.py:438
  17.4 0.2 collective-permute-start.4
  17.5 1.5 %collective-permute-start.5 = (f32[2,18,8,128]{3,2,1,0:T(8,128)S(1)}, f32[2,18,8,128]{3,2,1,0:T(8,128)S(1)}, u32[]{:S(2)}, u32[]{:S(2)}) collective-permute-start(f32[2,18,8,128]{3,2,1,0:T(8,128)S(1)} %get-tuple-element.39), channel_id=1, source_target_pairs={{0,2},{2,0},{1,3},{3,1},{4,6},{6,4},{5,7},{7,5},{8,10},{10,8},{9,1... | collective-permute-start | bytes 442376 | tf_op jit(solution)/shard_map/ppermute | solution.py:438
  19.0 0.8 %collective-permute-start.6 = (f32[8,128]{1,0:T(8,128)S(1)}, f32[8,128]{1,0:T(8,128)S(1)}, u32[]{:S(2)}, u32[]{:S(2)}) collective-permute-start(f32[8,128]{1,0:T(8,128)S(1)} %get-tuple-element.40.own), channel_id=1, source_target_pairs={{0,8},{4,12},{8,0},{12,4},{1,9},{5,13},{9,1},{13,5},{2,10},{6,14},... | collective-permute-start | bytes 12296 | tf_op jit(solution)/shard_map/ppermute | solution.py:438
  19.8 0.5 %shard_map.90.second = f32[18,8,128]{2,1,0:T(8,128)S(1)} custom-call(f32[2,18,8,128]{3,2,1,0:T(8,128)S(1)} %get-tuple-element.22.links, f32[8,72]{1,0:T(8,128)S(1)} %maximum_maximum_fusion.weights, f32[2,18,8,128]{3,2,1,0:T(8,128)S(1)} %get-tuple-element.28.cot), custom_call_target="tpu_custom_call" | custom-call | tf_op jit(solution)/shard_map/pallas_call | solution.py:425
  20.3 0.5 %shard_map.89.first = f32[18,8,128]{2,1,0:T(8,128)S(1)} custom-call(f32[2,18,8,128]{3,2,1,0:T(8,128)S(1)} %get-tuple-element.22.links, f32[8,72]{1,0:T(8,128)S(1)} %maximum_maximum_fusion.weights, f32[2,18,8,128]{3,2,1,0:T(8,128)S(1)} %get-tuple-element.28.cot), custom_call_target="tpu_custom_call" | custom-call | tf_op jit(solution)/shard_map/pallas_call | solution.py:425
  20.8 3.0 %collective-permute-done.6.opposite = f32[8,128]{1,0:T(8,128)S(1)} collective-permute-done((f32[8,128]{1,0:T(8,128)S(1)}, f32[8,128]{1,0:T(8,128)S(1)}, u32[]{:S(2)}, u32[]{:S(2)}) %collective-permute-start.6) | collective-permute-done | bytes 4128 | tf_op jit(solution)/shard_map/ppermute | solution.py:438
  23.9 0.0 collective-permute-done.3.t_next
  23.9 0.5 %collective-permute-done.4.t_prev = f32[37,8,128]{2,1,0:T(8,128)S(1)} collective-permute-done((f32[37,8,128]{2,1,0:T(8,128)S(1)}, f32[37,8,128]{2,1,0:T(8,128)S(1)}, u32[]{:S(2)}, u32[]{:S(2)}) %collective-permute-start.4) | collective-permute-done | bytes 151584 | tf_op jit(solution)/shard_map/ppermute | solution.py:438
  24.4 0.0 collective-permute-start.9
  24.4 1.5 %collective-permute-start.8 = (f32[8,128]{1,0:T(8,128)S(1)}, f32[8,128]{1,0:T(8,128)S(1)}, u32[]{:S(2)}, u32[]{:S(2)}) collective-permute-start(f32[8,128]{1,0:T(8,128)S(1)} %shard_map.92.refs_0_), channel_id=1, source_target_pairs={{0,2},{1,3},{2,0},{3,1},{4,6},{5,7},{6,4},{7,5},{8,10},{9,11},{10,... | collective-permute-start | bytes 12296 | tf_op jit(solution)/shard_map/ppermute | solution.py:452
  25.9 0.3 %collective-permute-start.7 = (f32[8,128]{1,0:T(8,128)S(1)}, f32[8,128]{1,0:T(8,128)S(1)}, u32[]{:S(2)}, u32[]{:S(2)}) collective-permute-start(f32[8,128]{1,0:T(8,128)S(1)} %shard_map.92.refs_0_), channel_id=1, source_target_pairs={{0,1},{1,0},{2,3},{3,2},{4,5},{5,4},{6,7},{7,6},{8,9},{9,8},{10,11... | collective-permute-start | bytes 12296 | tf_op jit(solution)/shard_map/ppermute | solution.py:452
  26.3 0.0 collective-permute-done.5.z_near
  26.3 1.0 %shard_map.91 = f32[2,18,8,128]{3,2,1,0:T(8,128)} custom-call(f32[2,18,8,128]{3,2,1,0:T(8,128)S(1)} %get-tuple-element.22.links, f32[8,72]{1,0:T(8,128)S(1)} %maximum_maximum_fusion.weights, f32[18,8,128]{2,1,0:T(8,128)S(1)} %shard_map.89.first, f32[18,8,128]{2,1,0:T(8,128)S(1)} %shard_map.90.second, f32[37,8,128]{2,1,0:T(8,128)S(1)} %collective-permute-done.3.t_next, ...), custom_call_target="tpu_custom_call" | custom-call | tf_op jit(solution)/shard_map/pallas_call | solution.py:425
  27.2 0.2 collective-permute-done.9.refs_3_
  27.5 0.6 %collective-permute-done.8.refs_2_ = f32[8,128]{1,0:T(8,128)S(1)} collective-permute-done((f32[8,128]{1,0:T(8,128)S(1)}, f32[8,128]{1,0:T(8,128)S(1)}, u32[]{:S(2)}, u32[]{:S(2)}) %collective-permute-start.8) | collective-permute-done | bytes 4128 | tf_op jit(solution)/shard_map/ppermute | solution.py:452
  28.1 0.0 collective-permute-done.7.refs_1_
  28.1 0.7 %shard_map.93 = f32[4,4,9]{2,1,0:T(4,128)} custom-call(f32[8,128]{1,0:T(8,128)S(1)} %shard_map.92.refs_0_, f32[8,128]{1,0:T(8,128)S(1)} %collective-permute-done.7.refs_1_, f32[8,128]{1,0:T(8,128)S(1)} %collective-permute-done.8.refs_2_, f32[8,128]{1,0:T(8,128)S(1)} %collective-permute-done.9.refs_3_), custom_call_target="tpu_custom_call" | custom-call | tf_op jit(solution)/shard_map/pallas_call | solution.py:425
  (1 shorter events, 0.0 us)
Async XLA Ops:
  0.6 9.7 %collective-permute-start = (f32[2,18,8,128]{3,2,1,0:T(8,128)}, f32[2,18,8,128]{3,2,1,0:T(8,128)S(1)}, u32[]{:S(2)}, u32[]{:S(2)}) collective-permute-start(f32[2,18,8,128]{3,2,1,0:T(8,128)} %bitcast.24), channel_id=1, source_target_pairs={{0,12},{4,0},{8,4},{12,8},{1,13},{5,1},{9,5},{13,9},{2,14},{6,2},{... | collective-permute-start | bytes 442376 | tf_op jit(solution)/shard_map/ppermute | solution.py:438
  5.7 2.9 %copy-start.1 = (f32[4,4,9]{2,1,0:T(4,128)S(1)}, f32[4,4,9]{2,1,0:T(4,128)}, u32[]{:S(2)}) copy-start(f32[4,4,9]{2,1,0:T(4,128)} %param.8) | copy-start | bytes 1732
  5.7 2.9 %copy-start.2 = (f32[4,4,4]{2,1,0:T(4,128)S(1)}, f32[4,4,4]{2,1,0:T(4,128)}, u32[]{:S(2)}) copy-start(f32[4,4,4]{2,1,0:T(4,128)} %constant.12) | copy-start | bytes 772
  5.7 2.9 %copy-start.3 = (f32[4,4,4]{2,1,0:T(4,128)S(1)}, f32[4,4,4]{2,1,0:T(4,128)}, u32[]{:S(2)}) copy-start(f32[4,4,4]{2,1,0:T(4,128)} %constant.11) | copy-start | bytes 772
  7.0 7.2 %collective-permute-start.1 = (f32[2,18,8,128]{3,2,1,0:T(8,128)S(1)}, f32[2,18,8,128]{3,2,1,0:T(8,128)S(1)}, u32[]{:S(2)}, u32[]{:S(2)}) collective-permute-start(f32[2,18,8,128]{3,2,1,0:T(8,128)S(1)} %get-tuple-element.25), channel_id=1, source_target_pairs={{0,4},{4,8},{8,12},{12,0},{1,5},{5,9},{9,13},{13,1},{2,6},{6,10},{... | collective-permute-start | bytes 442376 | tf_op jit(solution)/shard_map/ppermute | solution.py:438
  7.0 7.1 %collective-permute-start.2 = (f32[2,18,8,128]{3,2,1,0:T(8,128)S(1)}, f32[2,18,8,128]{3,2,1,0:T(8,128)S(1)}, u32[]{:S(2)}, u32[]{:S(2)}) collective-permute-start(f32[2,18,8,128]{3,2,1,0:T(8,128)S(1)} %get-tuple-element.26), channel_id=1, source_target_pairs={{0,2},{2,0},{1,3},{3,1},{4,6},{6,4},{5,7},{7,5},{8,10},{10,8},{9,1... | collective-permute-start | bytes 442376 | tf_op jit(solution)/shard_map/ppermute | solution.py:438
  10.2 3.9 %copy-start = (f32[1,1,2,256]{3,2,1,0:T(2,128)S(1)}, f32[1,1,2,256]{3,2,1,0:T(2,128)}, u32[]{:S(2)}) copy-start(f32[1,1,2,256]{3,2,1,0:T(2,128)} %param.9) | copy-start | bytes 6148
  15.4 8.4 %collective-permute-start.3 = (f32[37,8,128]{2,1,0:T(8,128)S(1)}, f32[37,8,128]{2,1,0:T(8,128)S(1)}, u32[]{:S(2)}, u32[]{:S(2)}) collective-permute-start(f32[37,8,128]{2,1,0:T(8,128)S(1)} %get-tuple-element.37), channel_id=1, source_target_pairs={{0,12},{4,0},{8,4},{12,8},{1,13},{5,1},{9,5},{13,9},{2,14},{6,2},{... | collective-permute-start | bytes 454664 | tf_op jit(solution)/shard_map/ppermute | solution.py:438
  17.4 7.0 %collective-permute-start.4 = (f32[37,8,128]{2,1,0:T(8,128)S(1)}, f32[37,8,128]{2,1,0:T(8,128)S(1)}, u32[]{:S(2)}, u32[]{:S(2)}) collective-permute-start(f32[37,8,128]{2,1,0:T(8,128)S(1)} %get-tuple-element.38), channel_id=1, source_target_pairs={{0,4},{4,8},{8,12},{12,0},{1,5},{5,9},{9,13},{13,1},{2,6},{6,10},{... | collective-permute-start | bytes 454664 | tf_op jit(solution)/shard_map/ppermute | solution.py:438
  17.5 8.7 %collective-permute-start.5 = (f32[2,18,8,128]{3,2,1,0:T(8,128)S(1)}, f32[2,18,8,128]{3,2,1,0:T(8,128)S(1)}, u32[]{:S(2)}, u32[]{:S(2)}) collective-permute-start(f32[2,18,8,128]{3,2,1,0:T(8,128)S(1)} %get-tuple-element.39), channel_id=1, source_target_pairs={{0,2},{2,0},{1,3},{3,1},{4,6},{6,4},{5,7},{7,5},{8,10},{10,8},{9,1... | collective-permute-start | bytes 442376 | tf_op jit(solution)/shard_map/ppermute | solution.py:438
  19.0 4.8 %collective-permute-start.6 = (f32[8,128]{1,0:T(8,128)S(1)}, f32[8,128]{1,0:T(8,128)S(1)}, u32[]{:S(2)}, u32[]{:S(2)}) collective-permute-start(f32[8,128]{1,0:T(8,128)S(1)} %get-tuple-element.40.own), channel_id=1, source_target_pairs={{0,8},{4,12},{8,0},{12,4},{1,9},{5,13},{9,1},{13,5},{2,10},{6,14},... | collective-permute-start | bytes 12296 | tf_op jit(solution)/shard_map/ppermute | solution.py:438
  24.4 3.1 %collective-permute-start.9 = (f32[8,128]{1,0:T(8,128)S(1)}, f32[8,128]{1,0:T(8,128)S(1)}, u32[]{:S(2)}, u32[]{:S(2)}) collective-permute-start(f32[8,128]{1,0:T(8,128)S(1)} %shard_map.92.refs_0_), channel_id=1, source_target_pairs={{0,3},{1,2},{2,1},{3,0},{4,7},{5,6},{6,5},{7,4},{8,11},{9,10},{10,... | collective-permute-start | bytes 12296 | tf_op jit(solution)/shard_map/ppermute | solution.py:452
  24.4 3.7 %collective-permute-start.8 = (f32[8,128]{1,0:T(8,128)S(1)}, f32[8,128]{1,0:T(8,128)S(1)}, u32[]{:S(2)}, u32[]{:S(2)}) collective-permute-start(f32[8,128]{1,0:T(8,128)S(1)} %shard_map.92.refs_0_), channel_id=1, source_target_pairs={{0,2},{1,3},{2,0},{3,1},{4,6},{5,7},{6,4},{7,5},{8,10},{9,11},{10,... | collective-permute-start | bytes 12296 | tf_op jit(solution)/shard_map/ppermute | solution.py:452
  25.9 2.2 %collective-permute-start.7 = (f32[8,128]{1,0:T(8,128)S(1)}, f32[8,128]{1,0:T(8,128)S(1)}, u32[]{:S(2)}, u32[]{:S(2)}) collective-permute-start(f32[8,128]{1,0:T(8,128)S(1)} %shard_map.92.refs_0_), channel_id=1, source_target_pairs={{0,1},{1,0},{2,3},{3,2},{4,5},{5,4},{6,7},{7,6},{8,9},{9,8},{10,11... | collective-permute-start | bytes 12296 | tf_op jit(solution)/shard_map/ppermute | solution.py:452

commit v3 on v2

--- a/solution.py
+++ b/solution.py
@@ -346,19 +346,22 @@
         ref[channel] = moved[first : first + NCH, :TERMS]
 
 
-def weight_partial(
-    out_in, field, cot, near, far, t_prev, z_near, *refs
-):
-    down, up, sums, out, spread, sem = refs[2:]
-    copy = pltpu.make_async_copy(out_in, out, sem)
-    copy.start()
+def weight_partial(field, cot, near, far, t_prev, z_near, *refs):
+    down, up, sums, spread = refs[2:]
     weight_sums((field, near, far, t_prev, z_near), cot, sums, spread)
     for ref in (down, up):
         ref[PLANES * COMPS] = sums[...]
+
+
+def near_backward(out_in, links, weights, cot, out, partial, sem):
+    copy = pltpu.make_async_copy(out_in, out, sem)
+    copy.start()
+    for plane in range(PLANES):
+        near_backward_plane(plane, links, weights, cot, partial)
     copy.wait()
 
 
-def near_backward(plane, links, weights, cot, partial):
+def near_backward_plane(plane, links, weights, cot, partial):
     turns = [turned(cot[plane, comp]) for comp in range(COMPS)]
 
     def mixed(term):
@@ -381,13 +384,13 @@
     other = mixed_items(weight_rows(weights, BACKWARD, term), load_items(cot, 1 - plane))
     add(hop_backward(link, other) if plane == 1 else hop_forward(link, other))
     for comp in range(COMPS):
-        partial[comp] = grads[comp]
-
-
-def far_backward(links, weights, first, second, t_next, t_prev, z_near, grad, held, sems):
+        partial[plane, comp] = grads[comp]
+
+
+def far_backward(links, weights, partial, t_next, t_prev, z_near, grad, held, sems):
     copies = []
-    for plane, partial in enumerate((first, second)):
-        grads = [partial[comp] for comp in range(COMPS)]
+    for plane in range(PLANES):
+        grads = load_items(partial, plane)
 
         def add(hop):
             for comp in range(COMPS):
@@ -510,10 +513,9 @@
         t_prev,
         z_near,
     )
-    down, up, sums, out = run(
+    down, up, sums = run(
         weight_partial,
-        (MESSAGE, MESSAGE, TILE, FIELD),
-        out,
+        (MESSAGE, MESSAGE, TILE),
         field,
         cot,
         near,
@@ -522,9 +524,8 @@
         z_near,
         down,
         up,
-        scratch=[pltpu.VMEM((NCH,) + FIELD, F32), pltpu.SemaphoreType.DMA],
-        out_hbm=(3,),
-        aliases=((7, 0), (8, 1)),
+        scratch=[pltpu.VMEM((NCH,) + FIELD, F32)],
+        aliases=((6, 0), (7, 1)),
     )
     t_next_cot = shifted(down, "ta", -1)
     t_prev_cot = shifted(up, "ta", 1)
@@ -533,11 +534,17 @@
         opposite = shifted(sums, "ta", 2)
     else:
         sums = paired_total(partners(sums, ("ta",)))
-    halves = [
-        run(functools.partial(near_backward, plane), (FIELD[1:],), links, weights, cot)[0]
-        for plane in range(PLANES)
-    ]
-    sums, *halves = lax.optimization_barrier((sums, *halves))
+    out, partial = run(
+        near_backward,
+        (FIELD, FIELD),
+        out,
+        links,
+        weights,
+        cot,
+        scratch=[pltpu.SemaphoreType.DMA],
+        out_hbm=(0,),
+    )
+    sums, partial = lax.optimization_barrier((sums, partial))
     if lax.axis_size("ta") == 4:
         (sums,) = run(line_sums, (TILE,), sums, opposite, t_next_cot, t_prev_cot)
     count = loss_weight.size
@@ -553,7 +560,7 @@
         (FIELD,),
         links,
         weights,
-        *halves,
+        partial,
         t_next_cot,
         t_prev_cot,
         z_near_cot,

time: 28.9 us -> 28.8 us (level)
    pallas_call x9 -> x8, Pallas kernels: 6.19 us -> 6.31 us  [run(): pl.pallas_call(kernel, out_shape=[jax.ShapeDtypeStruct(shape, F32) for sh...]
where the time goes in v3:
time: 28.8 us; the launch traced here: 28.7 us
  starting transfers between devices  12.9 us (45%)
  waiting for transfers between devices  8.14 us (28%)
  Pallas kernels  6.31 us (22%)
  between operations  0.71 us (2%)
  local copies, waits for them, and re-layouts  0.41 us (1%)
    ppermute x7, starting transfers between devices, shifted(): lax.ppermute(value, axis, [(i, (i + offset) % count) for i in range(count)])  11 us
    ppermute x7, waiting for transfers between devices, shifted(): lax.ppermute(value, axis, [(i, (i + offset) % count) for i in range(count)])  7.31 us
    pallas_call x8, Pallas kernels, run(): pl.pallas_call(kernel, out_shape=[jax.ShapeDtypeStruct(shape, F32) for sh...  6.31 us
    ppermute x3, starting transfers between devices, partners(): lax.ppermute(value, axes, [(i, i ^ k) for i in range(4)])  1.86 us
    ppermute x3, waiting for transfers between devices, partners(): lax.ppermute(value, axes, [(i, i ^ k) for i in range(4)])  0.83 us
  transfers between devices with their start and end apart: 10, of which 6 were waited for; matrix products, arithmetic and copies ran while one was open for 2% of the time, Pallas kernels for 15%

profile of v3, /device:TPU:0, one launch (start us, length us, event | category | flops | bytes accessed | tf_op | source)
XLA Modules:
  0.0 28.7 jit_solution(17410698437601831288)
XLA Ops:
  0.6 5.1 %collective-permute-start = (f32[2,18,8,128]{3,2,1,0:T(8,128)}, f32[2,18,8,128]{3,2,1,0:T(8,128)S(1)}, u32[]{:S(2)}, u32[]{:S(2)}) collective-permute-start(f32[2,18,8,128]{3,2,1,0:T(8,128)} %bitcast.24), channel_id=1, source_target_pairs={{0,12},{4,0},{8,4},{12,8},{1,13},{5,1},{9,5},{13,9},{2,14},{6,2},{... | collective-permute-start | bytes 442376 | tf_op jit(solution)/shard_map/ppermute | solution.py:441
  5.7 0.0 copy-start.1
  5.7 0.0 copy-start.2
  5.7 0.0 copy-start.3
  5.7 1.2 %shard_map.85 = (f32[2,18,8,128]{3,2,1,0:T(8,128)S(1)}, f32[2,18,8,128]{3,2,1,0:T(8,128)S(1)}, f32[2,18,8,128]{3,2,1,0:T(8,128)S(1)}, f32[2,18,8,128]{3,2,1,0:T(8,128)S(1)}) custom-call(f32[2,18,8,128]{3,2,1,0:T(8,128)} %bitcast.25, f32[2,18,8,128]{3,2,1,0:T(8,128)} %bitcast.23), custom_call_target="tpu_custom_call" | custom-call | tf_op jit(solution)/shard_map/pallas_call | solution.py:428
  7.0 0.1 collective-permute-start.1
  7.0 1.6 %collective-permute-start.2 = (f32[2,18,8,128]{3,2,1,0:T(8,128)S(1)}, f32[2,18,8,128]{3,2,1,0:T(8,128)S(1)}, u32[]{:S(2)}, u32[]{:S(2)}) collective-permute-start(f32[2,18,8,128]{3,2,1,0:T(8,128)S(1)} %get-tuple-element.26), channel_id=1, source_target_pairs={{0,2},{2,0},{1,3},{3,1},{4,6},{6,4},{5,7},{7,5},{8,10},{10,8},{9,1... | collective-permute-start | bytes 442376 | tf_op jit(solution)/shard_map/ppermute | solution.py:441
  8.6 0.0 copy-done.1
  8.6 0.0 copy-done.2
  8.6 0.0 copy-done.3
  8.6 0.1 multiply_reduce_fusion.1
  8.7 0.1 copy.21
  8.8 0.1 reshape.44
  8.9 0.1 copy.22
  9.0 0.1 reshape.45
  9.1 0.1 maximum_maximum_fusion.weights
  9.2 1.0 %shard_map.86 = (f32[2,18,8,128]{3,2,1,0:T(8,128)S(1)}, f32[5,2,18,8,128]{4,3,2,1,0:T(8,128)S(1)}) custom-call(f32[2,18,8,128]{3,2,1,0:T(8,128)S(1)} %get-tuple-element.23.field, f32[2,18,8,128]{3,2,1,0:T(8,128)S(1)} %get-tuple-element.22.links, f32[8,72]{1,0:T(8,128)S(1)} %maximum_maximum_fusion.weights), custom_call_target="tpu_custom_call" | custom-call | tf_op jit(solution)/shard_map/pallas_call | solution.py:428
  10.2 0.0 copy-start
  10.2 0.1 collective-permute-done.t_next
  10.3 3.8 %collective-permute-done.1.t_prev = f32[2,18,8,128]{3,2,1,0:T(8,128)S(1)} collective-permute-done((f32[2,18,8,128]{3,2,1,0:T(8,128)S(1)}, f32[2,18,8,128]{3,2,1,0:T(8,128)S(1)}, u32[]{:S(2)}, u32[]{:S(2)}) %collective-permute-start.1) | collective-permute-done | bytes 147488 | tf_op jit(solution)/shard_map/ppermute | solution.py:441
  14.1 0.0 collective-permute-done.2.z_near
  14.1 0.0 copy-done
  14.1 0.6 %shard_map.87 = (f32[2,18,8,128]{3,2,1,0:T(8,128)S(1)}, f32[2,18,8,128]{3,2,1,0:T(8,128)S(1)}, f32[3,18,8,128]{3,2,1,0:T(8,128)S(1)}, f32[37,8,128]{2,1,0:T(8,12...) custom-call(f32[2,18,8,128]{3,2,1,0:T(8,128)S(1)} %get-tuple-element.22.links, ...), custom_call_target="tpu_custom_call" | custom-call | tf_op jit(solution)/shard_map/pallas_call | solution.py:428
  14.8 0.6 %shard_map.89 = (f32[37,8,128]{2,1,0:T(8,128)S(1)}, f32[37,8,128]{2,1,0:T(8,128)S(1)}, f32[8,128]{1,0:T(8,128)S(1)}) custom-call(f32[2,18,8,128]{3,2,1,0:T(8,128)S(1)} %get-tuple-element.23.field, f32[2,18,8,128]{3,2,1,0:T(8,128)S(1)} %get-tuple-element.28.cot, ...), custom_call_target="tpu_custom_call", output_to_operand_aliasing={{0}: (6, {}), {1}: (7, {})} | custom-call | tf_op jit(solution)/shard_map/pallas_call | solution.py:428
  15.4 1.9 %collective-permute-start.3 = (f32[37,8,128]{2,1,0:T(8,128)S(1)}, f32[37,8,128]{2,1,0:T(8,128)S(1)}, u32[]{:S(2)}, u32[]{:S(2)}) collective-permute-start(f32[37,8,128]{2,1,0:T(8,128)S(1)} %get-tuple-element.37), channel_id=1, source_target_pairs={{0,12},{4,0},{8,4},{12,8},{1,13},{5,1},{9,5},{13,9},{2,14},{6,2},{... | collective-permute-start | bytes 454664 | tf_op jit(solution)/shard_map/ppermute | solution.py:441
  17.3 0.2 collective-permute-start.4
  17.4 1.5 %collective-permute-start.5 = (f32[2,18,8,128]{3,2,1,0:T(8,128)S(1)}, f32[2,18,8,128]{3,2,1,0:T(8,128)S(1)}, u32[]{:S(2)}, u32[]{:S(2)}) collective-permute-start(f32[2,18,8,128]{3,2,1,0:T(8,128)S(1)} %get-tuple-element.39), channel_id=1, source_target_pairs={{0,2},{2,0},{1,3},{3,1},{4,6},{6,4},{5,7},{7,5},{8,10},{10,8},{9,1... | collective-permute-start | bytes 442376 | tf_op jit(solution)/shard_map/ppermute | solution.py:441
  18.9 0.8 %collective-permute-start.6 = (f32[8,128]{1,0:T(8,128)S(1)}, f32[8,128]{1,0:T(8,128)S(1)}, u32[]{:S(2)}, u32[]{:S(2)}) collective-permute-start(f32[8,128]{1,0:T(8,128)S(1)} %get-tuple-element.40.own), channel_id=1, source_target_pairs={{0,8},{4,12},{8,0},{12,4},{1,9},{5,13},{9,1},{13,5},{2,10},{6,14},... | collective-permute-start | bytes 12296 | tf_op jit(solution)/shard_map/ppermute | solution.py:441
  19.7 1.2 %shard_map.88 = (f32[2,18,8,128]{3,2,1,0:T(8,128)}, f32[2,18,8,128]{3,2,1,0:T(8,128)S(1)}) custom-call(f32[2,18,8,128]{3,2,1,0:T(8,128)S(1)} %get-tuple-element.27.out_in, f32[2,18,8,128]{3,2,1,0:T(8,128)S(1)} %get-tuple-element.22.links, f32[8,72]{1,0:T(8,128)S(1)} %maximum_maximum_fusion.weights, f32[2,18,8,128]{3,2,1,0:T(8,128)S(1)} %get-tuple-element.28.cot), custom_call_target="tpu_custom_call" | custom-call | tf_op jit(solution)/shard_map/pallas_call | solution.py:428
  20.9 2.9 %collective-permute-done.6.opposite = f32[8,128]{1,0:T(8,128)S(1)} collective-permute-done((f32[8,128]{1,0:T(8,128)S(1)}, f32[8,128]{1,0:T(8,128)S(1)}, u32[]{:S(2)}, u32[]{:S(2)}) %collective-permute-start.6) | collective-permute-done | bytes 4128 | tf_op jit(solution)/shard_map/ppermute | solution.py:441
  23.8 0.0 collective-permute-done.3.t_next
  23.8 0.5 %collective-permute-done.4.t_prev = f32[37,8,128]{2,1,0:T(8,128)S(1)} collective-permute-done((f32[37,8,128]{2,1,0:T(8,128)S(1)}, f32[37,8,128]{2,1,0:T(8,128)S(1)}, u32[]{:S(2)}, u32[]{:S(2)}) %collective-permute-start.4) | collective-permute-done | bytes 151584 | tf_op jit(solution)/shard_map/ppermute | solution.py:441
  24.3 0.0 collective-permute-start.9
  24.3 1.5 %collective-permute-start.8 = (f32[8,128]{1,0:T(8,128)S(1)}, f32[8,128]{1,0:T(8,128)S(1)}, u32[]{:S(2)}, u32[]{:S(2)}) collective-permute-start(f32[8,128]{1,0:T(8,128)S(1)} %shard_map.91.refs_0_), channel_id=1, source_target_pairs={{0,2},{1,3},{2,0},{3,1},{4,6},{5,7},{6,4},{7,5},{8,10},{9,11},{10,... | collective-permute-start | bytes 12296 | tf_op jit(solution)/shard_map/ppermute | solution.py:455
  25.8 0.3 %collective-permute-start.7 = (f32[8,128]{1,0:T(8,128)S(1)}, f32[8,128]{1,0:T(8,128)S(1)}, u32[]{:S(2)}, u32[]{:S(2)}) collective-permute-start(f32[8,128]{1,0:T(8,128)S(1)} %shard_map.91.refs_0_), channel_id=1, source_target_pairs={{0,1},{1,0},{2,3},{3,2},{4,5},{5,4},{6,7},{7,6},{8,9},{9,8},{10,11... | collective-permute-start | bytes 12296 | tf_op jit(solution)/shard_map/ppermute | solution.py:455
  26.2 0.0 collective-permute-done.5.z_near
  26.2 1.0 %shard_map.90 = f32[2,18,8,128]{3,2,1,0:T(8,128)} custom-call(f32[2,18,8,128]{3,2,1,0:T(8,128)S(1)} %get-tuple-element.22.links, f32[8,72]{1,0:T(8,128)S(1)} %maximum_maximum_fusion.weights, f32[2,18,8,128]{3,2,1,0:T(8,128)S(1)} %get-tuple-element.36.partial, f32[37,8,128]{2,1,0:T(8,128)S(1)} %collective-permute-done.3.t_next, ...), custom_call_target="tpu_custom_call" | custom-call | tf_op jit(solution)/shard_map/pallas_call | solution.py:428
  27.2 0.2 collective-permute-done.9.refs_3_
  27.4 0.6 %collective-permute-done.8.refs_2_ = f32[8,128]{1,0:T(8,128)S(1)} collective-permute-done((f32[8,128]{1,0:T(8,128)S(1)}, f32[8,128]{1,0:T(8,128)S(1)}, u32[]{:S(2)}, u32[]{:S(2)}) %collective-permute-start.8) | collective-permute-done | bytes 4128 | tf_op jit(solution)/shard_map/ppermute | solution.py:455
  28.0 0.0 collective-permute-done.7.refs_1_
  28.0 0.7 %shard_map.92 = f32[4,4,9]{2,1,0:T(4,128)} custom-call(f32[8,128]{1,0:T(8,128)S(1)} %shard_map.91.refs_0_, f32[8,128]{1,0:T(8,128)S(1)} %collective-permute-done.7.refs_1_, f32[8,128]{1,0:T(8,128)S(1)} %collective-permute-done.8.refs_2_, f32[8,128]{1,0:T(8,128)S(1)} %collective-permute-done.9.refs_3_), custom_call_target="tpu_custom_call" | custom-call | tf_op jit(solution)/shard_map/pallas_call | solution.py:428
  (1 shorter events, 0.0 us)
Async XLA Ops:
  0.6 9.7 %collective-permute-start = (f32[2,18,8,128]{3,2,1,0:T(8,128)}, f32[2,18,8,128]{3,2,1,0:T(8,128)S(1)}, u32[]{:S(2)}, u32[]{:S(2)}) collective-permute-start(f32[2,18,8,128]{3,2,1,0:T(8,128)} %bitcast.24), channel_id=1, source_target_pairs={{0,12},{4,0},{8,4},{12,8},{1,13},{5,1},{9,5},{13,9},{2,14},{6,2},{... | collective-permute-start | bytes 442376 | tf_op jit(solution)/shard_map/ppermute | solution.py:441
  5.7 2.9 %copy-start.1 = (f32[4,4,9]{2,1,0:T(4,128)S(1)}, f32[4,4,9]{2,1,0:T(4,128)}, u32[]{:S(2)}) copy-start(f32[4,4,9]{2,1,0:T(4,128)} %param.8) | copy-start | bytes 1732
  5.7 2.9 %copy-start.2 = (f32[4,4,4]{2,1,0:T(4,128)S(1)}, f32[4,4,4]{2,1,0:T(4,128)}, u32[]{:S(2)}) copy-start(f32[4,4,4]{2,1,0:T(4,128)} %constant.12) | copy-start | bytes 772
  5.7 2.9 %copy-start.3 = (f32[4,4,4]{2,1,0:T(4,128)S(1)}, f32[4,4,4]{2,1,0:T(4,128)}, u32[]{:S(2)}) copy-start(f32[4,4,4]{2,1,0:T(4,128)} %constant.11) | copy-start | bytes 772
  7.0 7.2 %collective-permute-start.1 = (f32[2,18,8,128]{3,2,1,0:T(8,128)S(1)}, f32[2,18,8,128]{3,2,1,0:T(8,128)S(1)}, u32[]{:S(2)}, u32[]{:S(2)}) collective-permute-start(f32[2,18,8,128]{3,2,1,0:T(8,128)S(1)} %get-tuple-element.25), channel_id=1, source_target_pairs={{0,4},{4,8},{8,12},{12,0},{1,5},{5,9},{9,13},{13,1},{2,6},{6,10},{... | collective-permute-start | bytes 442376 | tf_op jit(solution)/shard_map/ppermute | solution.py:441
  7.0 7.1 %collective-permute-start.2 = (f32[2,18,8,128]{3,2,1,0:T(8,128)S(1)}, f32[2,18,8,128]{3,2,1,0:T(8,128)S(1)}, u32[]{:S(2)}, u32[]{:S(2)}) collective-permute-start(f32[2,18,8,128]{3,2,1,0:T(8,128)S(1)} %get-tuple-element.26), channel_id=1, source_target_pairs={{0,2},{2,0},{1,3},{3,1},{4,6},{6,4},{5,7},{7,5},{8,10},{10,8},{9,1... | collective-permute-start | bytes 442376 | tf_op jit(solution)/shard_map/ppermute | solution.py:441
  10.2 3.9 %copy-start = (f32[1,1,2,256]{3,2,1,0:T(2,128)S(1)}, f32[1,1,2,256]{3,2,1,0:T(2,128)}, u32[]{:S(2)}) copy-start(f32[1,1,2,256]{3,2,1,0:T(2,128)} %param.9) | copy-start | bytes 6148
  15.4 8.4 %collective-permute-start.3 = (f32[37,8,128]{2,1,0:T(8,128)S(1)}, f32[37,8,128]{2,1,0:T(8,128)S(1)}, u32[]{:S(2)}, u32[]{:S(2)}) collective-permute-start(f32[37,8,128]{2,1,0:T(8,128)S(1)} %get-tuple-element.37), channel_id=1, source_target_pairs={{0,12},{4,0},{8,4},{12,8},{1,13},{5,1},{9,5},{13,9},{2,14},{6,2},{... | collective-permute-start | bytes 454664 | tf_op jit(solution)/shard_map/ppermute | solution.py:441
  17.3 7.0 %collective-permute-start.4 = (f32[37,8,128]{2,1,0:T(8,128)S(1)}, f32[37,8,128]{2,1,0:T(8,128)S(1)}, u32[]{:S(2)}, u32[]{:S(2)}) collective-permute-start(f32[37,8,128]{2,1,0:T(8,128)S(1)} %get-tuple-element.38), channel_id=1, source_target_pairs={{0,4},{4,8},{8,12},{12,0},{1,5},{5,9},{9,13},{13,1},{2,6},{6,10},{... | collective-permute-start | bytes 454664 | tf_op jit(solution)/shard_map/ppermute | solution.py:441
  17.4 8.7 %collective-permute-start.5 = (f32[2,18,8,128]{3,2,1,0:T(8,128)S(1)}, f32[2,18,8,128]{3,2,1,0:T(8,128)S(1)}, u32[]{:S(2)}, u32[]{:S(2)}) collective-permute-start(f32[2,18,8,128]{3,2,1,0:T(8,128)S(1)} %get-tuple-element.39), channel_id=1, source_target_pairs={{0,2},{2,0},{1,3},{3,1},{4,6},{6,4},{5,7},{7,5},{8,10},{10,8},{9,1... | collective-permute-start | bytes 442376 | tf_op jit(solution)/shard_map/ppermute | solution.py:441
  18.9 4.8 %collective-permute-start.6 = (f32[8,128]{1,0:T(8,128)S(1)}, f32[8,128]{1,0:T(8,128)S(1)}, u32[]{:S(2)}, u32[]{:S(2)}) collective-permute-start(f32[8,128]{1,0:T(8,128)S(1)} %get-tuple-element.40.own), channel_id=1, source_target_pairs={{0,8},{4,12},{8,0},{12,4},{1,9},{5,13},{9,1},{13,5},{2,10},{6,14},... | collective-permute-start | bytes 12296 | tf_op jit(solution)/shard_map/ppermute | solution.py:441
  24.3 3.1 %collective-permute-start.9 = (f32[8,128]{1,0:T(8,128)S(1)}, f32[8,128]{1,0:T(8,128)S(1)}, u32[]{:S(2)}, u32[]{:S(2)}) collective-permute-start(f32[8,128]{1,0:T(8,128)S(1)} %shard_map.91.refs_0_), channel_id=1, source_target_pairs={{0,3},{1,2},{2,1},{3,0},{4,7},{5,6},{6,5},{7,4},{8,11},{9,10},{10,... | collective-permute-start | bytes 12296 | tf_op jit(solution)/shard_map/ppermute | solution.py:455
  24.3 3.7 %collective-permute-start.8 = (f32[8,128]{1,0:T(8,128)S(1)}, f32[8,128]{1,0:T(8,128)S(1)}, u32[]{:S(2)}, u32[]{:S(2)}) collective-permute-start(f32[8,128]{1,0:T(8,128)S(1)} %shard_map.91.refs_0_), channel_id=1, source_target_pairs={{0,2},{1,3},{2,0},{3,1},{4,6},{5,7},{6,4},{7,5},{8,10},{9,11},{10,... | collective-permute-start | bytes 12296 | tf_op jit(solution)/shard_map/ppermute | solution.py:455
  25.8 2.2 %collective-permute-start.7 = (f32[8,128]{1,0:T(8,128)S(1)}, f32[8,128]{1,0:T(8,128)S(1)}, u32[]{:S(2)}, u32[]{:S(2)}) collective-permute-start(f32[8,128]{1,0:T(8,128)S(1)} %shard_map.91.refs_0_), channel_id=1, source_target_pairs={{0,1},{1,0},{2,3},{3,2},{4,5},{5,4},{6,7},{7,6},{8,9},{9,8},{10,11... | collective-permute-start | bytes 12296 | tf_op jit(solution)/shard_map/ppermute | solution.py:455

commit v4 on v3

--- a/solution.py
+++ b/solution.py
@@ -257,9 +257,7 @@
         store_items(z_send, plane, items)
 
 
-def far_forward(
-    links, weights, loss, partial, t_next, t_prev, z_near, out, cot, terms, down, up, z_send
-):
+def early_forward(links, weights, partial, t_next, sums_out, terms):
     for plane in range(PLANES):
         sums = load_items(partial, plane)
 
@@ -268,16 +266,30 @@
             for comp in range(COMPS):
                 sums[comp] = sums[comp] + mixed[comp]
 
+        hop = hop_forward(load_link(links, plane, 0), load_items(t_next, plane))
+        store_items(terms, plane, hop)
+        add(1, hop)
+        store_items(sums_out, plane, sums)
+
+
+def far_forward(
+    links, weights, loss, partial, t_prev, z_near, out, cot, term_three, down, up, z_send
+):
+    for plane in range(PLANES):
+        sums = load_items(partial, plane)
+
+        def add(term, hop):
+            mixed = mixed_items(weight_rows(weights, FORWARD, term), hop)
+            for comp in range(COMPS):
+                sums[comp] = sums[comp] + mixed[comp]
+
         if plane == 0:
             add(4, load_items(z_near, 1))
         else:
             hop = hop_forward(load_link(links, 1, 1), load_items(z_near, 0))
-            store_items(terms, 2, hop)
+            for comp in range(COMPS):
+                term_three[comp] = hop[comp]
             add(3, hop)
-        t_link = load_link(links, plane, 0)
-        hop = hop_forward(t_link, load_items(t_next, plane))
-        store_items(terms, plane, hop)
-        add(1, hop)
         add(2, load_items(t_prev, plane))
         row = loss[plane : plane + 1, :]
         scale = jnp.where(
@@ -290,17 +302,18 @@
         store_items(cot, plane, cots)
         turns = [turned(item) for item in cots]
 
-        def pulled(direction, link):
+        def pulled(direction):
             rows = weight_rows(weights, BACKWARD, 2 * direction + 1)
-            return hop_backward(link, [mixed_item(rows, turn) for turn in turns])
+            items = [mixed_item(rows, turn) for turn in turns]
+            return hop_backward(load_link(links, plane, direction), items)
 
         store_message(down, plane, cots)
-        store_message(up, plane, pulled(0, t_link))
-        store_items(z_send, plane, pulled(1, load_link(links, 1, 1)) if plane == 1 else cots)
+        store_message(up, plane, pulled(0))
+        store_items(z_send, plane, pulled(1) if plane == 1 else cots)
 
 
 def term_item(sources, term, plane, comp):
-    field, near, far, t_prev, z_near = sources
+    field, near, far, three, t_prev, z_near = sources
     if term == 0:
         return field[plane, comp]
     if term == 1:
@@ -311,7 +324,7 @@
         return near[term - 5, plane, comp]
     if (term == 3) == (plane == 0):
         return near[4, plane, comp]
-    return far[2, comp] if term == 3 else z_near[1, comp]
+    return three[comp] if term == 3 else z_near[1, comp]
 
 
 def weight_sums(sources, cot, sums, spread):
@@ -346,9 +359,9 @@
         ref[channel] = moved[first : first + NCH, :TERMS]
 
 
-def weight_partial(field, cot, near, far, t_prev, z_near, *refs):
+def weight_partial(field, cot, near, far, three, t_prev, z_near, *refs):
     down, up, sums, spread = refs[2:]
-    weight_sums((field, near, far, t_prev, z_near), cot, sums, spread)
+    weight_sums((field, near, far, three, t_prev, z_near), cot, sums, spread)
     for ref in (down, up):
         ref[PLANES * COMPS] = sums[...]
 
@@ -502,14 +515,21 @@
     weights = weight_table(conv_weights)
     loss = loss_weight.reshape(PLANES, HALF * LANES)
     partial, near = run(near_forward, (FIELD, (5,) + FIELD), field, links, weights)
-    out, cot, far, down, up, z_send = run(
+    partial, far = run(
+        early_forward,
+        (FIELD, FIELD),
+        links,
+        weights,
+        partial,
+        t_next,
+    )
+    out, cot, three, down, up, z_send = run(
         far_forward,
-        (FIELD, FIELD, (3,) + FIELD[1:], MESSAGE, MESSAGE, FIELD),
+        (FIELD, FIELD, FIELD[1:], MESSAGE, MESSAGE, FIELD),
         links,
         weights,
         loss,
         partial,
-        t_next,
         t_prev,
         z_near,
     )
@@ -520,12 +540,13 @@
         cot,
         near,
         far,
+        three,
         t_prev,
         z_near,
         down,
         up,
         scratch=[pltpu.VMEM((NCH,) + FIELD, F32)],
-        aliases=((6, 0), (7, 1)),
+        aliases=((7, 0), (8, 1)),
     )
     t_next_cot = shifted(down, "ta", -1)
     t_prev_cot = shifted(up, "ta", 1)

time: 28.8 us -> 28.6 us (level)
    pallas_call x8 -> x9, Pallas kernels: 6.31 us -> 6.3 us  [run(): pl.pallas_call(kernel, out_shape=[jax.ShapeDtypeStruct(shape, F32) for sh...]
  transfers between devices with their start and end apart: 10 -> 10, of which waited for: 6 -> 6; matrix products, arithmetic and copies ran while one was open for 2% -> 2% of each run, Pallas kernels for 15% -> 16%
where the time goes in v4:
time: 28.6 us; the launch traced here: 28.5 us
  starting transfers between devices  12.9 us (45%)
  waiting for transfers between devices  7.96 us (28%)
  Pallas kernels  6.3 us (22%)
  between operations  0.71 us (2%)
  local copies, waits for them, and re-layouts  0.41 us (1%)
    ppermute x7, starting transfers between devices, shifted(): lax.ppermute(value, axis, [(i, (i + offset) % count) for i in range(count)])  11 us
    ppermute x7, waiting for transfers between devices, shifted(): lax.ppermute(value, axis, [(i, (i + offset) % count) for i in range(count)])  7.13 us
    pallas_call x9, Pallas kernels, run(): pl.pallas_call(kernel, out_shape=[jax.ShapeDtypeStruct(shape, F32) for sh...  6.3 us
    ppermute x3, starting transfers between devices, partners(): lax.ppermute(value, axes, [(i, i ^ k) for i in range(4)])  1.86 us
    ppermute x3, waiting for transfers between devices, partners(): lax.ppermute(value, axes, [(i, i ^ k) for i in range(4)])  0.83 us
  transfers between devices with their start and end apart: 10, of which 6 were waited for; matrix products, arithmetic and copies ran while one was open for 2% of the time, Pallas kernels for 16%

profile of v4, /device:TPU:0, one launch (start us, length us, event | category | flops | bytes accessed | tf_op | source)
XLA Modules:
  0.0 28.5 jit_solution(15826760517791018172)
XLA Ops:
  0.6 5.1 %collective-permute-start = (f32[2,18,8,128]{3,2,1,0:T(8,128)}, f32[2,18,8,128]{3,2,1,0:T(8,128)S(1)}, u32[]{:S(2)}, u32[]{:S(2)}) collective-permute-start(f32[2,18,8,128]{3,2,1,0:T(8,128)} %bitcast.24), channel_id=1, source_target_pairs={{0,12},{4,0},{8,4},{12,8},{1,13},{5,1},{9,5},{13,9},{2,14},{6,2},{... | collective-permute-start | bytes 442376 | tf_op jit(solution)/shard_map/ppermute | solution.py:454
  5.7 0.0 copy-start.1
  5.7 0.0 copy-start.2
  5.7 0.0 copy-start.3
  5.7 1.2 %shard_map.85 = (f32[2,18,8,128]{3,2,1,0:T(8,128)S(1)}, f32[2,18,8,128]{3,2,1,0:T(8,128)S(1)}, f32[2,18,8,128]{3,2,1,0:T(8,128)S(1)}, f32[2,18,8,128]{3,2,1,0:T(8,128)S(1)}) custom-call(f32[2,18,8,128]{3,2,1,0:T(8,128)} %bitcast.25, f32[2,18,8,128]{3,2,1,0:T(8,128)} %bitcast.23), custom_call_target="tpu_custom_call" | custom-call | tf_op jit(solution)/shard_map/pallas_call | solution.py:441
  7.0 0.1 collective-permute-start.1
  7.0 1.6 %collective-permute-start.2 = (f32[2,18,8,128]{3,2,1,0:T(8,128)S(1)}, f32[2,18,8,128]{3,2,1,0:T(8,128)S(1)}, u32[]{:S(2)}, u32[]{:S(2)}) collective-permute-start(f32[2,18,8,128]{3,2,1,0:T(8,128)S(1)} %get-tuple-element.29), channel_id=1, source_target_pairs={{0,2},{2,0},{1,3},{3,1},{4,6},{6,4},{5,7},{7,5},{8,10},{10,8},{9,1... | collective-permute-start | bytes 442376 | tf_op jit(solution)/shard_map/ppermute | solution.py:454
  8.6 0.0 copy-done.1
  8.6 0.0 copy-done.2
  8.6 0.0 copy-done.3
  8.6 0.1 multiply_reduce_fusion.1
  8.7 0.1 copy.21
  8.8 0.1 reshape.44
  8.9 0.1 copy.22
  9.0 0.1 reshape.45
  9.1 0.1 maximum_maximum_fusion.weights
  9.2 1.0 %shard_map.86 = (f32[2,18,8,128]{3,2,1,0:T(8,128)S(1)}, f32[5,2,18,8,128]{4,3,2,1,0:T(8,128)S(1)}) custom-call(f32[2,18,8,128]{3,2,1,0:T(8,128)S(1)} %get-tuple-element.25.field, f32[2,18,8,128]{3,2,1,0:T(8,128)S(1)} %get-tuple-element.24.links, f32[8,72]{1,0:T(8,128)S(1)} %maximum_maximum_fusion.weights), custom_call_target="tpu_custom_call" | custom-call | tf_op jit(solution)/shard_map/pallas_call | solution.py:441
  10.2 0.1 collective-permute-done.t_next
  10.3 0.2 shard_map.87
  10.5 0.0 copy-start
  10.5 3.6 %collective-permute-done.1.t_prev = f32[2,18,8,128]{3,2,1,0:T(8,128)S(1)} collective-permute-done((f32[2,18,8,128]{3,2,1,0:T(8,128)S(1)}, f32[2,18,8,128]{3,2,1,0:T(8,128)S(1)}, u32[]{:S(2)}, u32[]{:S(2)}) %collective-permute-start.1) | collective-permute-done | bytes 147488 | tf_op jit(solution)/shard_map/ppermute | solution.py:454
  14.1 0.0 collective-permute-done.2.z_near
  14.1 0.0 copy-done
  14.1 0.4 %shard_map.88 = (f32[2,18,8,128]{3,2,1,0:T(8,128)S(1)}, f32[2,18,8,128]{3,2,1,0:T(8,128)S(1)}, f32[18,8,128]{2,1,0:T(8,128)S(1)}, f32[37,8,128]{2,1,0:T(8,128)S(...) custom-call(f32[2,18,8,128]{3,2,1,0:T(8,128)S(1)} %get-tuple-element.24.links, ...), custom_call_target="tpu_custom_call" | custom-call | tf_op jit(solution)/shard_map/pallas_call | solution.py:441
  14.6 0.6 %shard_map.90 = (f32[37,8,128]{2,1,0:T(8,128)S(1)}, f32[37,8,128]{2,1,0:T(8,128)S(1)}, f32[8,128]{1,0:T(8,128)S(1)}) custom-call(f32[2,18,8,128]{3,2,1,0:T(8,128)S(1)} %get-tuple-element.25.field, f32[2,18,8,128]{3,2,1,0:T(8,128)S(1)} %get-tuple-element.31.cot, ...), custom_call_target="tpu_custom_call", output_to_operand_aliasing={{0}: (7, {}), {1}: (8, {})} | custom-call | tf_op jit(solution)/shard_map/pallas_call | solution.py:441
  15.2 1.9 %collective-permute-start.3 = (f32[37,8,128]{2,1,0:T(8,128)S(1)}, f32[37,8,128]{2,1,0:T(8,128)S(1)}, u32[]{:S(2)}, u32[]{:S(2)}) collective-permute-start(f32[37,8,128]{2,1,0:T(8,128)S(1)} %get-tuple-element.41), channel_id=1, source_target_pairs={{0,12},{4,0},{8,4},{12,8},{1,13},{5,1},{9,5},{13,9},{2,14},{6,2},{... | collective-permute-start | bytes 454664 | tf_op jit(solution)/shard_map/ppermute | solution.py:454
  17.1 0.2 collective-permute-start.4
  17.3 1.5 %collective-permute-start.5 = (f32[2,18,8,128]{3,2,1,0:T(8,128)S(1)}, f32[2,18,8,128]{3,2,1,0:T(8,128)S(1)}, u32[]{:S(2)}, u32[]{:S(2)}) collective-permute-start(f32[2,18,8,128]{3,2,1,0:T(8,128)S(1)} %get-tuple-element.43), channel_id=1, source_target_pairs={{0,2},{2,0},{1,3},{3,1},{4,6},{6,4},{5,7},{7,5},{8,10},{10,8},{9,1... | collective-permute-start | bytes 442376 | tf_op jit(solution)/shard_map/ppermute | solution.py:454
  18.8 0.8 %collective-permute-start.6 = (f32[8,128]{1,0:T(8,128)S(1)}, f32[8,128]{1,0:T(8,128)S(1)}, u32[]{:S(2)}, u32[]{:S(2)}) collective-permute-start(f32[8,128]{1,0:T(8,128)S(1)} %get-tuple-element.44.own), channel_id=1, source_target_pairs={{0,8},{4,12},{8,0},{12,4},{1,9},{5,13},{9,1},{13,5},{2,10},{6,14},... | collective-permute-start | bytes 12296 | tf_op jit(solution)/shard_map/ppermute | solution.py:454
  19.5 1.2 %shard_map.89 = (f32[2,18,8,128]{3,2,1,0:T(8,128)}, f32[2,18,8,128]{3,2,1,0:T(8,128)S(1)}) custom-call(f32[2,18,8,128]{3,2,1,0:T(8,128)S(1)} %get-tuple-element.30.out_in, f32[2,18,8,128]{3,2,1,0:T(8,128)S(1)} %get-tuple-element.24.links, f32[8,72]{1,0:T(8,128)S(1)} %maximum_maximum_fusion.weights, f32[2,18,8,128]{3,2,1,0:T(8,128)S(1)} %get-tuple-element.31.cot), custom_call_target="tpu_custom_call" | custom-call | tf_op jit(solution)/shard_map/pallas_call | solution.py:441
  20.7 2.9 %collective-permute-done.6.opposite = f32[8,128]{1,0:T(8,128)S(1)} collective-permute-done((f32[8,128]{1,0:T(8,128)S(1)}, f32[8,128]{1,0:T(8,128)S(1)}, u32[]{:S(2)}, u32[]{:S(2)}) %collective-permute-start.6) | collective-permute-done | bytes 4128 | tf_op jit(solution)/shard_map/ppermute | solution.py:454
  23.6 0.0 collective-permute-done.3.t_next
  23.6 0.5 %collective-permute-done.4.t_prev = f32[37,8,128]{2,1,0:T(8,128)S(1)} collective-permute-done((f32[37,8,128]{2,1,0:T(8,128)S(1)}, f32[37,8,128]{2,1,0:T(8,128)S(1)}, u32[]{:S(2)}, u32[]{:S(2)}) %collective-permute-start.4) | collective-permute-done | bytes 151584 | tf_op jit(solution)/shard_map/ppermute | solution.py:454
  24.1 0.0 collective-permute-start.9
  24.1 1.5 %collective-permute-start.8 = (f32[8,128]{1,0:T(8,128)S(1)}, f32[8,128]{1,0:T(8,128)S(1)}, u32[]{:S(2)}, u32[]{:S(2)}) collective-permute-start(f32[8,128]{1,0:T(8,128)S(1)} %shard_map.92.refs_0_), channel_id=1, source_target_pairs={{0,2},{1,3},{2,0},{3,1},{4,6},{5,7},{6,4},{7,5},{8,10},{9,11},{10,... | collective-permute-start | bytes 12296 | tf_op jit(solution)/shard_map/ppermute | solution.py:468
  25.6 0.3 %collective-permute-start.7 = (f32[8,128]{1,0:T(8,128)S(1)}, f32[8,128]{1,0:T(8,128)S(1)}, u32[]{:S(2)}, u32[]{:S(2)}) collective-permute-start(f32[8,128]{1,0:T(8,128)S(1)} %shard_map.92.refs_0_), channel_id=1, source_target_pairs={{0,1},{1,0},{2,3},{3,2},{4,5},{5,4},{6,7},{7,6},{8,9},{9,8},{10,11... | collective-permute-start | bytes 12296 | tf_op jit(solution)/shard_map/ppermute | solution.py:468
  26.0 0.0 collective-permute-done.5.z_near
  26.0 1.0 %shard_map.91 = f32[2,18,8,128]{3,2,1,0:T(8,128)} custom-call(f32[2,18,8,128]{3,2,1,0:T(8,128)S(1)} %get-tuple-element.24.links, f32[8,72]{1,0:T(8,128)S(1)} %maximum_maximum_fusion.weights, f32[2,18,8,128]{3,2,1,0:T(8,128)S(1)} %get-tuple-element.40.partial, f32[37,8,128]{2,1,0:T(8,128)S(1)} %collective-permute-done.3.t_next, ...), custom_call_target="tpu_custom_call" | custom-call | tf_op jit(solution)/shard_map/pallas_call | solution.py:441
  27.0 0.2 collective-permute-done.9.refs_3_
  27.2 0.6 %collective-permute-done.8.refs_2_ = f32[8,128]{1,0:T(8,128)S(1)} collective-permute-done((f32[8,128]{1,0:T(8,128)S(1)}, f32[8,128]{1,0:T(8,128)S(1)}, u32[]{:S(2)}, u32[]{:S(2)}) %collective-permute-start.8) | collective-permute-done | bytes 4128 | tf_op jit(solution)/shard_map/ppermute | solution.py:468
  27.8 0.0 collective-permute-done.7.refs_1_
  27.8 0.7 %shard_map.93 = f32[4,4,9]{2,1,0:T(4,128)} custom-call(f32[8,128]{1,0:T(8,128)S(1)} %shard_map.92.refs_0_, f32[8,128]{1,0:T(8,128)S(1)} %collective-permute-done.7.refs_1_, f32[8,128]{1,0:T(8,128)S(1)} %collective-permute-done.8.refs_2_, f32[8,128]{1,0:T(8,128)S(1)} %collective-permute-done.9.refs_3_), custom_call_target="tpu_custom_call" | custom-call | tf_op jit(solution)/shard_map/pallas_call | solution.py:441
  (1 shorter events, 0.0 us)
Async XLA Ops:
  0.6 9.7 %collective-permute-start = (f32[2,18,8,128]{3,2,1,0:T(8,128)}, f32[2,18,8,128]{3,2,1,0:T(8,128)S(1)}, u32[]{:S(2)}, u32[]{:S(2)}) collective-permute-start(f32[2,18,8,128]{3,2,1,0:T(8,128)} %bitcast.24), channel_id=1, source_target_pairs={{0,12},{4,0},{8,4},{12,8},{1,13},{5,1},{9,5},{13,9},{2,14},{6,2},{... | collective-permute-start | bytes 442376 | tf_op jit(solution)/shard_map/ppermute | solution.py:454
  5.7 2.9 %copy-start.1 = (f32[4,4,9]{2,1,0:T(4,128)S(1)}, f32[4,4,9]{2,1,0:T(4,128)}, u32[]{:S(2)}) copy-start(f32[4,4,9]{2,1,0:T(4,128)} %param.8) | copy-start | bytes 1732
  5.7 2.9 %copy-start.2 = (f32[4,4,4]{2,1,0:T(4,128)S(1)}, f32[4,4,4]{2,1,0:T(4,128)}, u32[]{:S(2)}) copy-start(f32[4,4,4]{2,1,0:T(4,128)} %constant.12) | copy-start | bytes 772
  5.7 2.9 %copy-start.3 = (f32[4,4,4]{2,1,0:T(4,128)S(1)}, f32[4,4,4]{2,1,0:T(4,128)}, u32[]{:S(2)}) copy-start(f32[4,4,4]{2,1,0:T(4,128)} %constant.11) | copy-start | bytes 772
  7.0 7.2 %collective-permute-start.1 = (f32[2,18,8,128]{3,2,1,0:T(8,128)S(1)}, f32[2,18,8,128]{3,2,1,0:T(8,128)S(1)}, u32[]{:S(2)}, u32[]{:S(2)}) collective-permute-start(f32[2,18,8,128]{3,2,1,0:T(8,128)S(1)} %get-tuple-element.28), channel_id=1, source_target_pairs={{0,4},{4,8},{8,12},{12,0},{1,5},{5,9},{9,13},{13,1},{2,6},{6,10},{... | collective-permute-start | bytes 442376 | tf_op jit(solution)/shard_map/ppermute | solution.py:454
  7.0 7.1 %collective-permute-start.2 = (f32[2,18,8,128]{3,2,1,0:T(8,128)S(1)}, f32[2,18,8,128]{3,2,1,0:T(8,128)S(1)}, u32[]{:S(2)}, u32[]{:S(2)}) collective-permute-start(f32[2,18,8,128]{3,2,1,0:T(8,128)S(1)} %get-tuple-element.29), channel_id=1, source_target_pairs={{0,2},{2,0},{1,3},{3,1},{4,6},{6,4},{5,7},{7,5},{8,10},{10,8},{9,1... | collective-permute-start | bytes 442376 | tf_op jit(solution)/shard_map/ppermute | solution.py:454
  10.5 3.6 %copy-start = (f32[1,1,2,256]{3,2,1,0:T(2,128)S(1)}, f32[1,1,2,256]{3,2,1,0:T(2,128)}, u32[]{:S(2)}) copy-start(f32[1,1,2,256]{3,2,1,0:T(2,128)} %param.9) | copy-start | bytes 6148
  15.2 8.4 %collective-permute-start.3 = (f32[37,8,128]{2,1,0:T(8,128)S(1)}, f32[37,8,128]{2,1,0:T(8,128)S(1)}, u32[]{:S(2)}, u32[]{:S(2)}) collective-permute-start(f32[37,8,128]{2,1,0:T(8,128)S(1)} %get-tuple-element.41), channel_id=1, source_target_pairs={{0,12},{4,0},{8,4},{12,8},{1,13},{5,1},{9,5},{13,9},{2,14},{6,2},{... | collective-permute-start | bytes 454664 | tf_op jit(solution)/shard_map/ppermute | solution.py:454
  17.1 7.0 %collective-permute-start.4 = (f32[37,8,128]{2,1,0:T(8,128)S(1)}, f32[37,8,128]{2,1,0:T(8,128)S(1)}, u32[]{:S(2)}, u32[]{:S(2)}) collective-permute-start(f32[37,8,128]{2,1,0:T(8,128)S(1)} %get-tuple-element.42), channel_id=1, source_target_pairs={{0,4},{4,8},{8,12},{12,0},{1,5},{5,9},{9,13},{13,1},{2,6},{6,10},{... | collective-permute-start | bytes 454664 | tf_op jit(solution)/shard_map/ppermute | solution.py:454
  17.3 8.7 %collective-permute-start.5 = (f32[2,18,8,128]{3,2,1,0:T(8,128)S(1)}, f32[2,18,8,128]{3,2,1,0:T(8,128)S(1)}, u32[]{:S(2)}, u32[]{:S(2)}) collective-permute-start(f32[2,18,8,128]{3,2,1,0:T(8,128)S(1)} %get-tuple-element.43), channel_id=1, source_target_pairs={{0,2},{2,0},{1,3},{3,1},{4,6},{6,4},{5,7},{7,5},{8,10},{10,8},{9,1... | collective-permute-start | bytes 442376 | tf_op jit(solution)/shard_map/ppermute | solution.py:454
  18.8 4.8 %collective-permute-start.6 = (f32[8,128]{1,0:T(8,128)S(1)}, f32[8,128]{1,0:T(8,128)S(1)}, u32[]{:S(2)}, u32[]{:S(2)}) collective-permute-start(f32[8,128]{1,0:T(8,128)S(1)} %get-tuple-element.44.own), channel_id=1, source_target_pairs={{0,8},{4,12},{8,0},{12,4},{1,9},{5,13},{9,1},{13,5},{2,10},{6,14},... | collective-permute-start | bytes 12296 | tf_op jit(solution)/shard_map/ppermute | solution.py:454
  24.1 3.1 %collective-permute-start.9 = (f32[8,128]{1,0:T(8,128)S(1)}, f32[8,128]{1,0:T(8,128)S(1)}, u32[]{:S(2)}, u32[]{:S(2)}) collective-permute-start(f32[8,128]{1,0:T(8,128)S(1)} %shard_map.92.refs_0_), channel_id=1, source_target_pairs={{0,3},{1,2},{2,1},{3,0},{4,7},{5,6},{6,5},{7,4},{8,11},{9,10},{10,... | collective-permute-start | bytes 12296 | tf_op jit(solution)/shard_map/ppermute | solution.py:468
  24.1 3.7 %collective-permute-start.8 = (f32[8,128]{1,0:T(8,128)S(1)}, f32[8,128]{1,0:T(8,128)S(1)}, u32[]{:S(2)}, u32[]{:S(2)}) collective-permute-start(f32[8,128]{1,0:T(8,128)S(1)} %shard_map.92.refs_0_), channel_id=1, source_target_pairs={{0,2},{1,3},{2,0},{3,1},{4,6},{5,7},{6,4},{7,5},{8,10},{9,11},{10,... | collective-permute-start | bytes 12296 | tf_op jit(solution)/shard_map/ppermute | solution.py:468
  25.6 2.2 %collective-permute-start.7 = (f32[8,128]{1,0:T(8,128)S(1)}, f32[8,128]{1,0:T(8,128)S(1)}, u32[]{:S(2)}, u32[]{:S(2)}) collective-permute-start(f32[8,128]{1,0:T(8,128)S(1)} %shard_map.92.refs_0_), channel_id=1, source_target_pairs={{0,1},{1,0},{2,3},{3,2},{4,5},{5,4},{6,7},{7,6},{8,9},{9,8},{10,11... | collective-permute-start | bytes 12296 | tf_op jit(solution)/shard_map/ppermute | solution.py:468
